TPU v7x, 512 devices: a whole 4x4x16 slice. The times are simulated.
512 devices in a mesh: sky: 32 (over x, z_hi, core), tm: 16 (over z_lo, y).
Axes of the slice: x: 4, y: 4, z: 16 (z_hi: 4, z_lo: 4; z = z_hi * 4 + z_lo), core: 2. Of those that a mesh axis runs over, the one named last changes fastest.
Arguments:
- residuals: float32 [4194304], P(('sky', 'tm')), may hold values from -6 to 6
- weights: float32 [4194304], P(('sky', 'tm')), may hold values from 0.1 to 10
- source_partials: bfloat16 [5, 4194304], P(None, ('sky', 'tm')), may hold values from -1.5 to 1.5
- attitude_partials: bfloat16 [32, 4194304], P(None, ('sky', 'tm')), may hold values from -0.025 to 0.045
- source_index: int32 [4194304], P(('sky', 'tm')), may hold values from 0 to 4095, as said below
- tile_window: int32 [32768], P(('sky', 'tm')), may hold values from 0 to 2047, as said below
- sources: float32 [5, 131072], P(None, 'sky'), may hold values from -6 to 6
- attitude: float32 [2048, 32], P('tm'), may hold values from -6 to 6
- coupling: float32 [2048], P('tm'), may hold values from 1 to 4
Outputs:
- new_sources: float32 [5, 131072], P(None, 'sky')
- new_attitude: float32 [2048, 32], P('tm')
Inputs may be any that keep to these rules, and one draw needn't show every extreme that they name: source_index counts among the 4096 sources of the sky region of the device that holds the observation (devices ordered sky first, then tm). The tiles held by the device at tm index t have tile_window from t * 128 to (t + 1) * 128 - 1.
All inputs are finite; a program needn't handle non-finite values.
Results may differ from a plain program's by a relative error of at most 0.00039.
Values sent between devices are 32-bit elements; how exact they have to be, the bound alone decides.
A program may use at most 64 MiB of HBM per device.

v0:
```python
import jax
import jax.numpy as jnp
from jax import lax
from jax.sharding import PartitionSpec as P

TILE = 128
ITERS = 8


LOWER_PAIRS = tuple(((i, j) for i in range(5) for j in range(i + 1)))
DAMPING = 0.8
HIGHEST = lax.Precision.HIGHEST


def extended(block, sides, width):
    for axis, dim in sides:
        count = lax.axis_size(axis)
        forward = [(i, i + 1) for i in range(count - 1)]
        backward = [(target, source) for source, target in forward]
        low = lax.ppermute(
            lax.slice_in_dim(block, block.shape[dim] - width, None, axis=dim), axis, forward
        )
        high = lax.ppermute(lax.slice_in_dim(block, 0, width, axis=dim), axis, backward)
        block = jnp.concatenate([low, block, high], axis=dim)
    return block


def passed_along(x, axis, by):
    peers = lax.axis_size(axis)
    pairs = [(i, i + by) for i in range(peers) if 0 <= i + by < peers]
    return lax.ppermute(x, axis, pairs)


def moment_rows(partials, weights, residuals):
    values = partials.astype(jnp.float32)
    entries = [weights * values[i] * values[j] for i, j in LOWER_PAIRS]
    entries = entries + [weights * values[i] * residuals for i in range(5)]
    return jnp.stack(entries)


def solve_sources(moments):
    matrix = {}
    for position, pair in enumerate(LOWER_PAIRS):
        matrix[pair] = moments[position] + (1.0 if pair[0] == pair[1] else 0.0)
    factor = {}
    for i in range(5):
        for j in range(i + 1):
            reduced = matrix[i, j]
            for k in range(j):
                reduced = reduced - factor[i, k] * factor[j, k]
            if i == j:
                factor[i, i] = jnp.sqrt(reduced)
            else:
                factor[i, j] = reduced / factor[j, j]
    forward = []
    for i in range(5):
        current = moments[15 + i]
        for k in range(i):
            current = current - factor[i, k] * forward[k]
        forward.append(current / factor[i, i])
    result = [None] * 5
    for i in reversed(range(5)):
        current = forward[i]
        for k in range(i + 1, 5):
            current = current - factor[k, i] * result[k]
        result[i] = current / factor[i, i]
    return jnp.stack(result)


def window_inverse(symmetric, left_coupling, right_coupling):
    knot_count = symmetric.shape[1]
    identity = jnp.eye(knot_count, dtype=jnp.float32)
    blocks = symmetric + (left_coupling + right_coupling)[:, None, None] * identity
    lower_factor = jnp.linalg.cholesky(blocks)
    inverse_factor = jax.scipy.linalg.solve_triangular(
        lower_factor, jnp.broadcast_to(identity, blocks.shape), lower=True
    )
    return jnp.einsum("wlk,wlm->wkm", inverse_factor, inverse_factor, precision=HIGHEST)


def apply_blocks(blocks, vectors):
    return jnp.einsum("wkl,wl->wk", blocks, vectors, precision=HIGHEST)


def time_rim(values):
    return extended(values, (("tm", 0),), 1)


def sweep_step(change, symmetric, inverse, right_side, left_coupling, right_coupling, padded):
    applied = apply_blocks(symmetric, change) + (left_coupling + right_coupling)[:, None] * change
    applied = applied - left_coupling[:, None] * padded[:-2] - right_coupling[:, None] * padded[2:]
    return change + DAMPING * apply_blocks(inverse, right_side - applied)


def on_device(
    residuals,
    weights,
    source_partials,
    attitude_partials,
    source_index,
    tile_window,
    sources,
    attitude,
    coupling,
):
    source_count = sources.shape[1]
    window_count = attitude.shape[0]
    knot_count = attitude.shape[1]
    tile_count = attitude_partials.shape[1] // TILE
    summands = moment_rows(source_partials, weights, residuals)
    moments = jnp.zeros((20, source_count), jnp.float32).at[:, source_index].add(summands)
    scaled = (weights[None, :] * attitude_partials.astype(jnp.float32)).astype(jnp.bfloat16)
    shaped_att = attitude_partials.reshape(knot_count, tile_count, TILE)
    tile_normal = jnp.einsum(
        "ktp,ltp->tkl",
        scaled.reshape(knot_count, tile_count, TILE),
        shaped_att,
        preferred_element_type=jnp.float32,
    )
    tile_normal = tile_normal.reshape(tile_count, knot_count * knot_count)
    first_window = lax.axis_index("tm") * window_count
    window_ids = lax.broadcasted_iota(jnp.int32, (window_count, tile_count), 0)
    selector = (tile_window[None, :] - first_window == window_ids).astype(jnp.float32)
    normal_local = jnp.dot(selector, tile_normal, precision=HIGHEST)
    totals = lax.psum(moments, "tm")
    source_change = solve_sources(totals)
    new_sources = sources + source_change
    picked = source_change[:, source_index]
    corrected = residuals - jnp.sum(source_partials.astype(jnp.float32) * picked, axis=0)
    weighted = (weights * corrected).astype(jnp.bfloat16)
    tile_rhs = jnp.einsum(
        "ktp,tp->tk",
        shaped_att,
        weighted.reshape(tile_count, TILE),
        preferred_element_type=jnp.float32,
    )
    rhs_local = jnp.dot(selector, tile_rhs, precision=HIGHEST)
    previous = passed_along(coupling[-1:], "tm", 1)
    left_coupling = jnp.concatenate([previous, coupling[:-1]])
    is_final = lax.axis_index("tm") == lax.axis_size("tm") - 1
    final_slot = lax.broadcasted_iota(jnp.int32, (window_count,), 0) == window_count - 1
    right_coupling = jnp.where(jnp.logical_and(is_final, final_slot), 0.0, coupling)
    normal_sum, right_side = lax.psum((normal_local, rhs_local), "sky")
    normal = normal_sum.reshape(window_count, knot_count, knot_count)
    symmetric = 0.5 * (normal + jnp.swapaxes(normal, 1, 2))
    inverse = window_inverse(symmetric, left_coupling, right_coupling)
    change = DAMPING * apply_blocks(inverse, right_side)
    for sweep in range(ITERS - 1):
        padded = time_rim(change)
        change = sweep_step(
            change, symmetric, inverse, right_side, left_coupling, right_coupling, padded
        )
    return (new_sources, attitude + change)


def solution(mesh):
    return jax.shard_map(
        on_device,
        mesh=mesh,
        in_specs=(
            P(("sky", "tm")),
            P(("sky", "tm")),
            P(None, ("sky", "tm")),
            P(None, ("sky", "tm")),
            P(("sky", "tm")),
            P(("sky", "tm")),
            P(None, "sky"),
            P("tm", None),
            P("tm"),
        ),
        out_specs=(P(None, "sky"), P("tm", None)),
        check_vma=False,
    )
```

profile of v0, /device:TPU:24, one launch (start us, length us, event | category | flops | bytes accessed | tf_op | source)
XLA Modules:
  0.0 1118.4 jit_solution(11065479881714924849)
XLA Ops:
  9.4 9.9 slice_reduce_fusion
  20.1 2.4 stack.91
  22.5 2.6 copy.70
  25.2 45.7 %scatter_custom_fusion = f32[20,4096]{0,1:T(8,128)} fusion(s32[8192]{0:T(1024)S(1)} %get-tuple-element.56, f32[8192,20]{1,0:T(8,128)} %copy.70, f32[]{:T(128)} %constant.54.clone.1), kind=kCustom, calls=%fused_computation.32 | custom fusion | flops 163840 | bytes 328192 | tf_op jit(solution)/shard_map/scatter-add | solution.py:111
  70.9 3.0 copy.71
  74.6 3.9 collective-permute-start
  83.0 2.9 copy.76
  86.6 159.8 %all-reduce.3.cloned.1.call-done = f32[20,4096]{1,0:T(8,128)} async-done(((f32[20,4096]{1,0:T(8,128)}), f32[20,4096]{1,0:T(8,128)}) %all-reduce.3.cloned.1.call-update) | async-done | bytes 327696 | tf_op jit(solution)/shard_map/psum | solution.py:125
  246.4 2.5 fusion.83
  254.4 29.3 %gather_fusion = f32[8192,5]{1,0:T(8,128)} fusion(f32[5,4096]{0,1:T(8,128)} %copy.83, s32[8192]{0:T(1024)S(1)} %get-tuple-element.55), kind=kCustom, calls=%fused_computation | custom fusion | bytes 360448 | tf_op jit(solution)/shard_map/gather | solution.py:128
  283.7 3.4 fusion
  287.7 168.7 %psum.23 = f32[128,32]{0,1:T(8,128)S(1)} all-reduce(f32[128,32]{0,1:T(8,128)S(1)} %fusion.16), channel_id=1, replica_groups=mesh['sky'=32,'tm'=16] {'sky'}, use_global_device_ids=true, to_apply=%region_6.7 | all-reduce | flops 4096 | bytes 32768 | tf_op jit(solution)/shard_map/psum | solution.py:143
  457.2 150.4 %all-reduce.5.cloned.1.call-done = f32[128,32,32]{1,2,0:T(8,128)} async-done(((f32[128,32,32]{1,2,0:T(8,128)}), f32[128,32,32]{1,2,0:T(8,128)}) %all-reduce.5.cloned.1.call-update) | async-done | bytes 524304 | tf_op jit(solution)/shard_map/psum | solution.py:143
  607.6 2.9 copy.77
  610.5 3.9 multiply_add_fusion
  616.3 3.4 fusion.1
  619.6 375.5 %custom-call.8 = f32[128,32,32]{2,1,0:T(8,128)S(1)} custom-call(f32[128,32,32]{2,1,0:T(8,128)} %fusion.1), custom_call_target="Cholesky" | custom-call | tf_op jit(solution)/shard_map/jit(cholesky)/cholesky | solution.py:74
  996.9 12.5 %custom-call.9 = f32[128,1,32,32]{0,2,3,1:T(8,128)S(1)} custom-call(f32[128,1,32,32]{0,3,2,1:T(8,128)S(1)} %select_bitcast_fusion), custom_call_target="InvertDiagBlocksLowerTriangular" | custom-call | tf_op jit(solution)/shard_map/jit(_solve_triangular)/vmap()/triangular_solve | solution.py:75
  1013.2 4.0 multiply_reduce_fusion.14
  1019.4 4.1 collective-permute-start.2
  1030.4 2.7 collective-permute-start.3
  1033.2 3.1 collective-permute-start.4
  1036.4 4.6 collective-permute-done.4
  1046.1 3.9 collective-permute-start.6
  1050.1 3.8 collective-permute-done.6
  1059.1 3.9 collective-permute-start.8
  1063.1 3.8 collective-permute-done.8
  1072.0 6.0 collective-permute-start.9
  1082.8 6.3 collective-permute-start.11
  1091.1 5.8 collective-permute-done.12
  1102.1 3.9 collective-permute-start.14
  1106.1 3.8 collective-permute-done.14
  (131 shorter events, 60.9 us)
Async XLA Ops:
  7.2 239.3 %all-reduce.3.cloned.1.call-start = ((), (), s32[]{:S(2)}) async-start(), calls=%async_computation | async-start | bytes 786432 | tf_op jit(solution)/shard_map/psum | solution.py:125
  9.4 10.0 copy-start.1
  9.4 10.0 copy-start.3
  22.5 2.6 copy-start.4
  25.2 48.8 %copy-start.6 = (f32[128]{0:T(128)S(1)}, f32[128]{0:T(128)}, u32[]{:S(2)}) copy-start(f32[128]{0:T(128)} %param.17) | copy-start | bytes 1540
  70.9 9.2 copy-start.7
  73.9 533.7 %all-reduce.5.cloned.1.call-start = ((), (), s32[]{:S(2)}) async-start(), calls=%async_computation.1 | async-start | bytes 4194304 | tf_op jit(solution)/shard_map/psum | solution.py:143
  74.6 11.3 %collective-permute-start = (f32[1]{0:T(128)}, f32[1]{0:T(128)}, u32[]{:S(2)}, u32[]{:S(2)}) collective-permute-start(f32[1]{0:T(128)} %slice.246), channel_id=1, source_target_pairs={{0,1},{1,2},{2,3},{3,4},{4,5},{5,6},{6,7},{7,8},{8,9},{9,10},{10,1... | collective-permute-start | bytes 20 | tf_op jit(solution)/shard_map/ppermute | solution.py:31
  283.7 3.4 copy-start
  283.7 172.8 %copy-start.2 = (f32[5,4096]{1,0:T(8,128)S(1)}, f32[5,4096]{1,0:T(8,128)}, u32[]{:S(2)}) copy-start(f32[5,4096]{1,0:T(8,128)} %param.15) | copy-start | bytes 245764
  1017.5 8.3 collective-permute-start.1
  1019.4 7.7 collective-permute-start.2
  1030.4 5.9 collective-permute-start.3
  1033.2 7.7 collective-permute-start.4
  1044.2 5.9 collective-permute-start.5
  1046.1 7.7 collective-permute-start.6
  1057.2 5.9 collective-permute-start.7
  1059.1 7.7 collective-permute-start.8
  1070.1 8.0 collective-permute-start.10
  1072.0 7.5 collective-permute-start.9
  1082.8 8.3 collective-permute-start.11
  1089.1 7.7 collective-permute-start.12
  1097.9 12.8 %copy-start.5 = (f32[128,32]{0,1:T(8,128)S(1)}, f32[128,32]{0,1:T(8,128)}, u32[]{:S(2)}) copy-start(f32[128,32]{0,1:T(8,128)} %param.16) | copy-start | bytes 49156
  1100.2 5.9 collective-permute-start.13
  1102.1 7.7 collective-permute-start.14
Sparse Core Ops, SparseCore 0:
  74.1 172.3 all-reduce.2
  249.3 358.2 all-reduce.4
where the time goes:
time: 1130 us; the launch traced here: 1120 us
  other arithmetic  474 us (42%)
  waiting for transfers between devices  335 us (30%)
  blocking collectives  169 us (15%)
  local copies, waits for them, and re-layouts  67 us (6%)
  starting transfers between devices  49.6 us (4%)
  between operations  14.9 us (1%)
    another operation x4, other arithmetic, window_inverse(): lower_factor = jnp.linalg.cholesky(blocks)  376 us
    psum x1, blocking collectives, on_device(): normal_sum, right_side = lax.psum((normal_local, rhs_local), 'sky')  169 us
    psum x1, waiting for transfers between devices, on_device(): totals = lax.psum(moments, 'tm')  160 us
    psum x1, waiting for transfers between devices, on_device(): normal_sum, right_side = lax.psum((normal_local, rhs_local), 'sky')  150 us
    scatter-add x1, other arithmetic, on_device(): jnp.zeros((20, source_count), jnp.float32).at[:, source_index].add(summands)  45.7 us
    gather x1, local copies, waits for them, and re-layouts, on_device(): picked = source_change[:, source_index]  29.3 us
    ppermute x7, waiting for transfers between devices, extended(): lax.ppermute(lax.slice_in_dim(block, 0, width, axis=dim), axis, backward)  22.9 us
    ppermute x7, starting transfers between devices, extended(): lax.ppermute(lax.slice_in_dim(block, 0, width, axis=dim), axis, backward)  22.9 us
  transfers between devices with their start and end apart: 17, of which 9 were waited for; matrix products, arithmetic and copies ran while one was open for 5% of the time, Pallas kernels for 0%

commit v1 on v0

v1 whole, which is shorter than its diff:
```python
import functools

import jax
import jax.numpy as jnp
from jax import lax
from jax.experimental import pallas as pl
from jax.experimental.pallas import tpu as pltpu
from jax.sharding import PartitionSpec as P

TILE = 128
ITERS = 8
BLOCK = 8
LOWER_PAIRS = tuple(((i, j) for i in range(5) for j in range(i + 1)))
DAMPING = 0.8
HIGHEST = lax.Precision.HIGHEST
MESH = pl.DeviceIdType.MESH
VMEM = pl.BlockSpec(memory_space=pltpu.VMEM)


def along_time(count):
    return count, lambda: lax.axis_index("tm"), lambda p: {"tm": p}


def along_plane():
    def spot():
        sky = lax.axis_index("sky")
        return lax.div(sky, 8) * 2 + lax.rem(sky, 2)

    def name(p):
        depth = lax.rem(lax.div(lax.axis_index("sky"), 2), 4)
        return {"sky": lax.div(p, 2) * 8 + depth * 2 + lax.rem(p, 2)}

    return 8, spot, name


def along_depth():
    def spot():
        return lax.rem(lax.div(lax.axis_index("sky"), 2), 4)

    def name(p):
        sky = lax.axis_index("sky")
        return {"sky": lax.div(sky, 8) * 8 + p * 2 + lax.rem(sky, 2)}

    return 4, spot, name


def meet(count, me, name):
    barrier = pltpu.get_barrier_semaphore()
    for step in range(1, count):
        pl.semaphore_signal(
            barrier, inc=1, device_id=name(lax.rem(me + step, count)), device_id_type=MESH
        )
    pl.semaphore_wait(barrier, count - 1)


def sum_kernel(group, finish, x_ref, o_ref, land, send_sem, recv_sem):
    count, spot, name = group
    me = spot()
    meet(count, me, name)
    copies = []
    for step in range(1, count):
        peer = lax.rem(me + step, count)
        copy = pltpu.make_async_remote_copy(
            src_ref=x_ref.at[peer],
            dst_ref=land.at[step - 1],
            send_sem=send_sem.at[step - 1],
            recv_sem=recv_sem.at[step - 1],
            device_id=name(peer),
            device_id_type=MESH,
        )
        copy.start()
        copies.append(copy)
    total = x_ref[me]
    for step in range(1, count):
        copies[step - 1].wait_recv()
        total = total + land[step - 1]
    finish(total, o_ref)
    for copy in copies:
        copy.wait_send()


def spread_kernel(group, x_ref, o_ref, land, send_sem, recv_sem):
    count, spot, name = group
    me = spot()
    meet(count, me, name)
    copies = []
    for step in range(1, count):
        copy = pltpu.make_async_remote_copy(
            src_ref=x_ref,
            dst_ref=land.at[step - 1],
            send_sem=send_sem.at[step - 1],
            recv_sem=recv_sem.at[step - 1],
            device_id=name(lax.rem(me + step, count)),
            device_id_type=MESH,
        )
        copy.start()
        copies.append(copy)
    o_ref[me] = x_ref[...]
    for step in range(1, count):
        copies[step - 1].wait_recv()
        o_ref[lax.rem(me + count - step, count)] = land[step - 1]
    for copy in copies:
        copy.wait_send()


def group_call(kernel, name, count, x, block, out, collective_id):
    return pl.pallas_call(
        kernel,
        name=name,
        out_shape=jax.ShapeDtypeStruct(out, jnp.float32),
        in_specs=[VMEM],
        out_specs=VMEM,
        scratch_shapes=[
            pltpu.VMEM((count - 1,) + block, jnp.float32),
            pltpu.SemaphoreType.DMA((count - 1,)),
            pltpu.SemaphoreType.DMA((count - 1,)),
        ],
        compiler_params=pltpu.CompilerParams(collective_id=collective_id, has_side_effects=True),
    )(x)


def keep(total, o_ref):
    o_ref[...] = total


def summed(x, group, collective_id, finish=keep, rows=None):
    block = x.shape[1:]
    out = block if rows is None else (rows,) + block[1:]
    kernel = functools.partial(sum_kernel, group, finish)
    return group_call(kernel, "summed", group[0], x, block, out, collective_id)


def spread(x, group, collective_id):
    kernel = functools.partial(spread_kernel, group)
    return group_call(kernel, "spread", group[0], x, x.shape, (group[0],) + x.shape, collective_id)


def moment_rows(partials, weights, residuals):
    values = partials.astype(jnp.float32)
    entries = [weights * values[i] * values[j] for i, j in LOWER_PAIRS]
    entries = entries + [weights * values[i] * residuals for i in range(5)]
    return jnp.stack(entries)


def solve_sources(moments):
    matrix = {}
    for position, pair in enumerate(LOWER_PAIRS):
        matrix[pair] = moments[position] + (1.0 if pair[0] == pair[1] else 0.0)
    factor = {}
    for i in range(5):
        for j in range(i + 1):
            reduced = matrix[i, j]
            for k in range(j):
                reduced = reduced - factor[i, k] * factor[j, k]
            if i == j:
                factor[i, i] = jnp.sqrt(reduced)
            else:
                factor[i, j] = reduced / factor[j, j]
    forward = []
    for i in range(5):
        current = moments[15 + i]
        for k in range(i):
            current = current - factor[i, k] * forward[k]
        forward.append(current / factor[i, i])
    result = [None] * 5
    for i in reversed(range(5)):
        current = forward[i]
        for k in range(i + 1, 5):
            current = current - factor[k, i] * result[k]
        result[i] = current / factor[i, i]
    return result


def finish_sources(total, o_ref):
    solved = solve_sources([total[r : r + 1, :] for r in range(20)])
    zero = jnp.zeros_like(solved[0])
    o_ref[...] = jnp.concatenate(solved + [zero] * 3, axis=0)


def applied(inverse, vector, knots):
    parts = [None] * 4
    for row in range(knots):
        term = inverse[row] * vector[row : row + 1, :]
        spot = row % 4
        parts[spot] = term if parts[spot] is None else parts[spot] + term
    return (parts[0] + parts[1]) + (parts[2] + parts[3])


def attitude_kernel(
    knots, count, packed_ref, ties_ref, o_ref, inverse, sent, land, send_sem, recv_sem
):
    me = lax.axis_index("tm")
    after, before = lax.rem(me + 1, count), lax.rem(me + count - 1, count)
    barrier = pltpu.get_barrier_semaphore()
    for peer in (before, after):
        pl.semaphore_signal(barrier, inc=1, device_id={"tm": peer}, device_id_type=MESH)

    left, right = ties_ref[0:1, :], ties_ref[1:2, :]
    lanes = left.shape[1]
    row_ids = lax.broadcasted_iota(jnp.int32, (knots, lanes), 0)
    start = 0
    for group in range(knots // BLOCK):
        width = (group + 1) * BLOCK
        for k in range(group * BLOCK, width):
            row = packed_ref[start : start + width, :]
            row = row + jnp.where(row_ids[:width] == k, left + right, 0.0)
            inverse[k, :width, :] = row
            start += width
    for low in range(knots // BLOCK):
        for high in range(low + 1, knots // BLOCK):
            rows = pl.ds(high * BLOCK, BLOCK)
            for k in range(low * BLOCK, (low + 1) * BLOCK):
                inverse[k, rows, :] = inverse[rows, k, :]
    right_side = packed_ref[start : start + knots, :]

    def pivot(p, carry):
        own = inverse[p]
        here = row_ids == p
        scale = 1.0 / inverse[p, pl.ds(p, 1), :]
        row = jnp.where(here, scale, own * scale)
        for i in range(knots):
            factor = inverse[i, pl.ds(p, 1), :]
            inverse[i] = jnp.where(here, 0.0, inverse[i]) - factor * row
        inverse[p] = row
        return carry

    lax.fori_loop(0, knots, pivot, 0)

    base = DAMPING * applied(inverse, right_side, knots)
    lane_ids = lax.broadcasted_iota(jnp.int32, (knots, lanes), 1)
    change = base
    pl.semaphore_wait(barrier, 2)
    for sweep in range(ITERS - 1):
        sent[sweep] = change
        copies = []
        for side, peer in enumerate((after, before)):
            copy = pltpu.make_async_remote_copy(
                src_ref=sent.at[sweep],
                dst_ref=land.at[sweep, side],
                send_sem=send_sem.at[sweep, side],
                recv_sem=recv_sem.at[sweep, side],
                device_id={"tm": peer},
                device_id_type=MESH,
            )
            copy.start()
            copies.append(copy)
        own_low, own_high = pltpu.roll(change, 1, 1), pltpu.roll(change, lanes - 1, 1)
        for copy in copies:
            copy.wait()
        low = jnp.where(lane_ids == 0, pltpu.roll(land[sweep, 0], 1, 1), own_low)
        high = jnp.where(
            lane_ids == lanes - 1, pltpu.roll(land[sweep, 1], lanes - 1, 1), own_high
        )
        tied = left * low + right * high
        change = (1.0 - DAMPING) * change + base + DAMPING * applied(inverse, tied, knots)
    o_ref[...] = change


def attitude_change(packed, ties, knots, count):
    lanes = ties.shape[1]
    sweeps = ITERS - 1
    return pl.pallas_call(
        functools.partial(attitude_kernel, knots, count),
        name="attitude_change",
        out_shape=jax.ShapeDtypeStruct((knots, lanes), jnp.float32),
        in_specs=[VMEM, VMEM],
        out_specs=VMEM,
        scratch_shapes=[
            pltpu.VMEM((knots, knots, lanes), jnp.float32),
            pltpu.VMEM((sweeps, knots, lanes), jnp.float32),
            pltpu.VMEM((sweeps, 2, knots, lanes), jnp.float32),
            pltpu.SemaphoreType.DMA((sweeps, 2)),
            pltpu.SemaphoreType.DMA((sweeps, 2)),
        ],
        compiler_params=pltpu.CompilerParams(collective_id=7, has_side_effects=True),
    )(packed, ties)


def on_device(
    residuals,
    weights,
    source_partials,
    attitude_partials,
    source_index,
    tile_window,
    sources,
    attitude,
    coupling,
):
    source_count = sources.shape[1]
    window_count, knot_count = attitude.shape
    tile_count = attitude_partials.shape[1] // TILE
    times = lax.axis_size("tm")
    time_group = along_time(times)

    summands = moment_rows(source_partials, weights, residuals)
    moments = jnp.zeros((20, source_count), jnp.float32).at[:, source_index].add(summands)
    moments = moments.reshape(20, times, source_count // times).transpose(1, 0, 2)
    owned = summed(moments, time_group, 1, finish_sources, 8)
    source_change = spread(owned, time_group, 2)
    source_change = source_change[:, :5].transpose(1, 0, 2).reshape(5, source_count)
    new_sources = sources + source_change

    scaled = (weights[None, :] * attitude_partials.astype(jnp.float32)).astype(jnp.bfloat16)
    shaped_att = attitude_partials.reshape(knot_count, tile_count, TILE)
    tile_normal = jnp.einsum(
        "ktp,ltp->tkl",
        scaled.reshape(knot_count, tile_count, TILE),
        shaped_att,
        preferred_element_type=jnp.float32,
    )
    tile_normal = 0.5 * (tile_normal + jnp.swapaxes(tile_normal, 1, 2))
    tile_lower = jnp.concatenate(
        [
            tile_normal[:, b : b + BLOCK, : b + BLOCK].reshape(tile_count, -1)
            for b in range(0, knot_count, BLOCK)
        ],
        axis=1,
    )

    picked = source_change[:, source_index]
    corrected = residuals - jnp.sum(source_partials.astype(jnp.float32) * picked, axis=0)
    weighted = (weights * corrected).astype(jnp.bfloat16)
    tile_rhs = jnp.einsum(
        "ktp,tp->tk",
        shaped_att,
        weighted.reshape(tile_count, TILE),
        preferred_element_type=jnp.float32,
    )
    tile_rows = jnp.concatenate([tile_lower, tile_rhs], axis=1)
    first_window = lax.axis_index("tm") * window_count
    window_ids = lax.broadcasted_iota(jnp.int32, (tile_count, window_count), 1)
    selector = (tile_window[:, None] - first_window == window_ids).astype(jnp.float32)
    packed = lax.dot_general(
        tile_rows, selector, (((0,), (0,)), ((), ())), precision=HIGHEST
    )
    packed = jnp.pad(packed, ((0, 768 - packed.shape[0]), (0, 0)))

    plane, depth = along_plane(), along_depth()
    part = summed(packed.reshape(8, 96, window_count), plane, 3)
    part = summed(part.reshape(4, 24, window_count), depth, 4)
    part = spread(part, depth, 5).reshape(96, window_count)
    packed = spread(part, plane, 6).reshape(768, window_count)

    earlier = lax.ppermute(coupling[-1:], "tm", [(i, i + 1) for i in range(times - 1)])
    left = jnp.concatenate([earlier, coupling[:-1]])
    is_final = lax.axis_index("tm") == times - 1
    final_slot = lax.broadcasted_iota(jnp.int32, (window_count,), 0) == window_count - 1
    right = jnp.where(jnp.logical_and(is_final, final_slot), 0.0, coupling)
    change = attitude_change(packed, jnp.stack([left, right]), knot_count, times)
    return (new_sources, attitude + change.T)


def solution(mesh):
    return jax.shard_map(
        on_device,
        mesh=mesh,
        in_specs=(
            P(("sky", "tm")),
            P(("sky", "tm")),
            P(None, ("sky", "tm")),
            P(None, ("sky", "tm")),
            P(("sky", "tm")),
            P(("sky", "tm")),
            P(None, "sky"),
            P("tm", None),
            P("tm"),
        ),
        out_specs=(P(None, "sky"), P("tm", None)),
        check_vma=False,
    )
```

time: 1130 us -> 245 us (0.22)
  the two profiles are of different devices: /device:TPU:24 before, /device:TPU:4 now
where the time goes in v1:
time: 245 us; the launch traced here: 244 us
  Pallas kernels  125 us (51%)
  local copies, waits for them, and re-layouts  57.7 us (24%)
  other arithmetic  54.2 us (22%)
  starting transfers between devices  3.95 us (2%)
    pallas_call x6, Pallas kernels, group_call(): pl.pallas_call(kernel, name=name, out_shape=jax.ShapeDtypeStruct(out, jnp...  82.2 us
    scatter-add x1, other arithmetic, on_device(): jnp.zeros((20, source_count), jnp.float32).at[:, source_index].add(summands)  45.7 us
    pallas_call x1, Pallas kernels, attitude_change(): pl.pallas_call(functools.partial(attitude_kernel, knots, count), name='at...  42.7 us
    gather x1, local copies, waits for them, and re-layouts, on_device(): picked = source_change[:, source_index]  29.3 us
    slice x1, local copies, waits for them, and re-layouts, moment_rows(): entries = [weights * values[i] * values[j] for i, j in LOWER_PAIRS]  9.95 us
    another operation x2, local copies, waits for them, and re-layouts, moment_rows(): return jnp.stack(entries)  5.95 us
  transfers between devices with their start and end apart: 1, of which 0 were waited for; matrix products, arithmetic and copies ran while one was open for 45% of the time, Pallas kernels for 34%

profile of v1, /device:TPU:4, one launch (start us, length us, event | category | flops | bytes accessed | tf_op | source)
XLA Modules:
  0.0 244.1 jit_solution(5332899834431069265)
XLA Ops:
  0.6 1.2 slice.34
  1.9 3.9 %collective-permute-start = (f32[1]{0:T(128)}, f32[1]{0:T(128)}, u32[]{:S(2)}, u32[]{:S(2)}) collective-permute-start(f32[1]{0:T(128)} %slice.34), channel_id=1, source_target_pairs={{0,1},{1,2},{2,3},{3,4},{4,5},{5,6},{6,7},{7,8},{8,9},{9,10},{10,1... | collective-permute-start | bytes 20 | tf_op jit(solution)/shard_map/ppermute | solution.py:345
  5.8 1.6 fusion.7
  7.4 0.3 copy.23
  8.0 0.8 slice.85
  8.9 0.7 slice.87
  9.6 1.0 copy.17
  11.0 9.9 %slice_reduce_fusion = (f32[8192]{0:T(1024)S(1)}, f32[8192]{0:T(1024)S(1)}, f32[8192]{0:T(1024)S(1)}, f32[8192]{0:T(1024)S(1)}, f32[8192]{0:T(1024)S(1)}) fusion(f32[5,8192]{0,1:T(8,128)S(1)} %convert_element_type.16), kind=kLoop, calls=%fused_computation.2 | loop fusion | bytes 327680 | tf_op jit(solution)/shard_map/slice | solution.py:140
  20.9 0.7 multiply_multiply_fusion.5
  21.6 0.7 fusion.20
  22.3 3.3 %stack.92 = f32[20,8192]{1,0:T(8,128)S(1)} concatenate(f32[1,8192]{1,0:T(1,128)S(1)} %bitcast.96, f32[1,8192]{1,0:T(1,128)S(1)} %bitcast.93, f32[1,8192]{1,0:T(1,128)S(1)} %bitcast.92, f32[1,8192]{1,0:T(1,128)S(1)} %bitcast.94, f32[1,8192]{1,0:T(1,128)S(1)} %bitcast.90, f32[1,8192]{1,0:T(1,128)S(1)} %bitcast.97, f32[1,8192]{1,0:T(1,128)} %bitcast.107, f32[1,8192]{1,0:T(1,128)} %bitcast.105, ...), dimensions={0} | concatenate | bytes 1310720 | tf_op jit(solution)/shard_map/stack | solution.py:142
  25.6 2.6 %copy.18 = f32[8192,20]{1,0:T(8,128)} copy(f32[8192,20]{0,1:T(8,128)S(1)} %bitcast.78) | data formatting | bytes 1310720 | tf_op jit(solution)/shard_map/stack | solution.py:142
  28.3 45.7 %scatter_custom_fusion = f32[20,4096]{0,1:T(8,128)} fusion(s32[8192]{0:T(1024)S(1)} %get-tuple-element.27, f32[8192,20]{1,0:T(8,128)} %copy.18, f32[]{:T(128)} %constant.8.clone.1), kind=kCustom, calls=%fused_computation.12 | custom fusion | flops 163840 | bytes 328192 | tf_op jit(solution)/shard_map/scatter-add | solution.py:297
  74.0 3.0 %copy.20 = f32[20,16,256]{2,0,1:T(8,128)} copy(f32[20,16,256]{0,2,1:T(8,128)} %bitcast.77) | data formatting | bytes 655360 | tf_op jit(solution)/shard_map/reshape | solution.py:298
  77.0 15.0 %summed.3.x_ref = f32[8,256]{1,0:T(8,128)} custom-call(f32[16,20,256]{2,1,0:T(8,128)} %bitcast.81), custom_call_target="tpu_custom_call" | custom-call | tf_op jit(solution)/shard_map/summed/pallas_call | solution.py:107
  92.0 13.7 %spread.3 = f32[16,8,256]{2,1,0:T(8,128)} custom-call(f32[8,256]{1,0:T(8,128)} %summed.3.x_ref), custom_call_target="tpu_custom_call" | custom-call | tf_op jit(solution)/shard_map/spread/pallas_call | solution.py:107
  105.7 2.9 %copy.28 = f32[5,4096]{0,1:T(8,128)} copy(f32[5,4096]{1,0:T(8,128)} %bitcast.82) | data formatting | bytes 163840 | tf_op jit(solution)/shard_map/reshape | solution.py:301
  108.6 29.3 %gather_fusion = f32[8192,5]{1,0:T(8,128)} fusion(f32[5,4096]{0,1:T(8,128)} %copy.28, s32[8192]{0:T(1024)S(1)} %get-tuple-element.26), kind=kCustom, calls=%fused_computation | custom fusion | bytes 360448 | tf_op jit(solution)/shard_map/gather | solution.py:321
  138.0 3.4 %fusion = f32[8192]{0:T(1024)S(1)} fusion(f32[8192,5]{1,0:T(8,128)} %gather_fusion, bf16[5,8192]{0,1:T(8,128)(2,1)S(1)} %copy.17), kind=kLoop, calls=%fused_computation.8 | loop fusion | flops 114688 | bytes 278528 | tf_op jit(solution)/shard_map/reduce_sum | solution.py:322
  141.4 0.4 fusion.5
  141.9 1.1 copy.24
  143.5 0.4 fusion.14
  143.9 0.8 pad.4
  144.6 10.6 %summed.4 = f32[96,128]{1,0:T(8,128)} custom-call(f32[8,96,128]{2,1,0:T(8,128)} %bitcast.80), custom_call_target="tpu_custom_call" | custom-call | tf_op jit(solution)/shard_map/summed/pallas_call | solution.py:107
  155.3 17.6 %summed.5.x_ref = f32[24,128]{1,0:T(8,128)} custom-call(f32[4,24,128]{2,1,0:T(8,128)} %bitcast.87), custom_call_target="tpu_custom_call" | custom-call | tf_op jit(solution)/shard_map/summed/pallas_call | solution.py:107
  172.9 14.6 %spread.4 = f32[4,24,128]{2,1,0:T(8,128)} custom-call(f32[24,128]{1,0:T(8,128)} %summed.5.x_ref), custom_call_target="tpu_custom_call" | custom-call | tf_op jit(solution)/shard_map/spread/pallas_call | solution.py:107
  187.5 10.6 %spread.5 = f32[8,96,128]{2,1,0:T(8,128)} custom-call(f32[96,128]{1,0:T(8,128)} %bitcast.88), custom_call_target="tpu_custom_call" | custom-call | tf_op jit(solution)/shard_map/spread/pallas_call | solution.py:107
  198.1 0.7 add.18
  198.8 0.6 maximum_bitcast_fusion
  199.4 0.6 pad_maximum_fusion.ties_ref
  200.0 42.7 %attitude_change.1 = f32[32,128]{1,0:T(8,128)} custom-call(f32[768,128]{1,0:T(8,128)} %bitcast.79, f32[2,128]{1,0:T(2,128)} %pad_maximum_fusion.ties_ref), custom_call_target="tpu_custom_call" | custom-call | tf_op jit(solution)/shard_map/attitude_change/pallas_call | solution.py:262
  242.7 1.3 bitcast_add_fusion.1
  (43 shorter events, 1.2 us)
Async XLA Ops:
  1.9 196.9 %collective-permute-start = (f32[1]{0:T(128)}, f32[1]{0:T(128)}, u32[]{:S(2)}, u32[]{:S(2)}) collective-permute-start(f32[1]{0:T(128)} %slice.34), channel_id=1, source_target_pairs={{0,1},{1,2},{2,3},{3,4},{4,5},{5,6},{6,7},{7,8},{8,9},{9,10},{10,1... | collective-permute-start | bytes 20 | tf_op jit(solution)/shard_map/ppermute | solution.py:345
  7.4 2.2 copy-start.5
  8.0 2.9 %copy-start = (f32[64,32,32]{2,1,0:T(8,128)}, f32[64,32,32]{2,1,0:T(8,128)S(1)}, u32[]{:S(2)}) copy-start(f32[64,32,32]{2,1,0:T(8,128)S(1)} %fusion.1) | copy-start | bytes 786436
  10.9 10.0 %copy-start.4 = (f32[8192]{0:T(1024)S(1)}, f32[8192]{0:T(1024)}, u32[]{:S(2)}) copy-start(f32[8192]{0:T(1024)} %param.10) | copy-start | bytes 98308
  10.9 10.0 %copy-start.7 = (f32[8192]{0:T(1024)S(1)}, f32[8192]{0:T(1024)}, u32[]{:S(2)}) copy-start(f32[8192]{0:T(1024)} %param.9) | copy-start | bytes 98308
  25.6 2.6 %copy-start.8 = (s32[8192]{0:T(1024)S(1)}, s32[8192]{0:T(1024)}, u32[]{:S(2)}) copy-start(s32[8192]{0:T(1024)} %param.13) | copy-start | bytes 98308
  108.6 32.8 %copy-start.1 = (bf16[32,8192]{1,0:T(8,128)(2,1)S(1)}, bf16[32,8192]{1,0:T(8,128)(2,1)}, u32[]{:S(2)}) copy-start(bf16[32,8192]{1,0:T(8,128)(2,1)} %param.12) | copy-start | bytes 1572868
  138.0 5.1 %copy-start.3 = (f32[64,8,24]{2,1,0:T(8,128)S(1)}, f32[64,8,24]{2,1,0:T(8,128)}, u32[]{:S(2)}) copy-start(f32[64,8,24]{2,1,0:T(8,128)} %slice.87) | copy-start | bytes 147460
  138.0 5.3 %slice-start = ((f32[64,32,32]{2,1,0:T(8,128)}), f32[64,8,32]{2,1,0:T(8,128)S(1)}, s32[]{:S(2)}) async-start(f32[64,32,32]{2,1,0:T(8,128)} %copy-done), calls=%async_computation | async-start | bytes 524288 | tf_op jit(solution)/shard_map/slice | solution.py:315
  138.0 5.5 %copy-start.10 = (s32[64]{0:T(128)S(1)}, s32[64]{0:T(128)}, u32[]{:S(2)}) copy-start(s32[64]{0:T(128)} %param.14) | copy-start | bytes 772
  141.4 56.7 %copy-start.11 = (f32[128]{0:T(128)S(1)}, f32[128]{0:T(128)}, u32[]{:S(2)}) copy-start(f32[128]{0:T(128)} %param.17) | copy-start | bytes 1540
  141.4 56.7 %copy-start.2 = (f32[16,8,256]{2,1,0:T(8,128)S(1)}, f32[16,8,256]{2,1,0:T(8,128)}, u32[]{:S(2)}) copy-start(f32[16,8,256]{2,1,0:T(8,128)} %spread.3) | copy-start | bytes 393220
  141.4 56.7 %copy-start.6 = (f32[5,4096]{1,0:T(8,128)S(1)}, f32[5,4096]{1,0:T(8,128)}, u32[]{:S(2)}) copy-start(f32[5,4096]{1,0:T(8,128)} %param.15) | copy-start | bytes 245764
  141.4 101.3 %copy-start.9 = (f32[128,32]{0,1:T(8,128)S(1)}, f32[128,32]{0,1:T(8,128)}, u32[]{:S(2)}) copy-start(f32[128,32]{0,1:T(8,128)} %param.16) | copy-start | bytes 49156

commit v2 on v1

--- a/solution.py
+++ b/solution.py
@@ -10,6 +10,7 @@
 TILE = 128
 ITERS = 8
 BLOCK = 8
+PIECE = 24
 LOWER_PAIRS = tuple(((i, j) for i in range(5) for j in range(i + 1)))
 DAMPING = 0.8
 HIGHEST = lax.Precision.HIGHEST
@@ -44,24 +45,23 @@
     return 4, spot, name
 
 
-def meet(count, me, name):
-    barrier = pltpu.get_barrier_semaphore()
-    for step in range(1, count):
-        pl.semaphore_signal(
-            barrier, inc=1, device_id=name(lax.rem(me + step, count)), device_id_type=MESH
-        )
-    pl.semaphore_wait(barrier, count - 1)
-
-
-def sum_kernel(group, finish, x_ref, o_ref, land, send_sem, recv_sem):
+def signal_all(barrier, group):
     count, spot, name = group
     me = spot()
-    meet(count, me, name)
+    for step in range(1, count):
+        peer = lax.rem(me + step, count)
+        pl.semaphore_signal(barrier, inc=1, device_id=name(peer), device_id_type=MESH)
+    return count - 1
+
+
+def send_all(group, source, land, send_sem, recv_sem):
+    count, spot, name = group
+    me = spot()
     copies = []
     for step in range(1, count):
         peer = lax.rem(me + step, count)
         copy = pltpu.make_async_remote_copy(
-            src_ref=x_ref.at[peer],
+            src_ref=source(peer),
             dst_ref=land.at[step - 1],
             send_sem=send_sem.at[step - 1],
             recv_sem=recv_sem.at[step - 1],
@@ -70,76 +70,39 @@
         )
         copy.start()
         copies.append(copy)
-    total = x_ref[me]
-    for step in range(1, count):
-        copies[step - 1].wait_recv()
-        total = total + land[step - 1]
-    finish(total, o_ref)
+    return copies
+
+
+def sum_stage(group, x_ref, land, send_sem, recv_sem):
+    copies = send_all(group, lambda peer: x_ref.at[peer], land, send_sem, recv_sem)
+    total = x_ref[group[1]()]
+    for step, copy in enumerate(copies):
+        copy.wait_recv()
+        total = total + land[step]
     for copy in copies:
         copy.wait_send()
-
-
-def spread_kernel(group, x_ref, o_ref, land, send_sem, recv_sem):
-    count, spot, name = group
+    return total
+
+
+def spread_stage(group, x_ref, land, send_sem, recv_sem, place):
+    count, spot, _ = group
     me = spot()
-    meet(count, me, name)
-    copies = []
-    for step in range(1, count):
-        copy = pltpu.make_async_remote_copy(
-            src_ref=x_ref,
-            dst_ref=land.at[step - 1],
-            send_sem=send_sem.at[step - 1],
-            recv_sem=recv_sem.at[step - 1],
-            device_id=name(lax.rem(me + step, count)),
-            device_id_type=MESH,
-        )
-        copy.start()
-        copies.append(copy)
-    o_ref[me] = x_ref[...]
-    for step in range(1, count):
-        copies[step - 1].wait_recv()
-        o_ref[lax.rem(me + count - step, count)] = land[step - 1]
+    copies = send_all(group, lambda peer: x_ref, land, send_sem, recv_sem)
+    place(me, x_ref[...])
+    for step, copy in enumerate(copies):
+        copy.wait_recv()
+        place(lax.rem(me + count - step - 1, count), land[step])
     for copy in copies:
         copy.wait_send()
 
 
-def group_call(kernel, name, count, x, block, out, collective_id):
-    return pl.pallas_call(
-        kernel,
-        name=name,
-        out_shape=jax.ShapeDtypeStruct(out, jnp.float32),
-        in_specs=[VMEM],
-        out_specs=VMEM,
-        scratch_shapes=[
-            pltpu.VMEM((count - 1,) + block, jnp.float32),
-            pltpu.SemaphoreType.DMA((count - 1,)),
-            pltpu.SemaphoreType.DMA((count - 1,)),
-        ],
-        compiler_params=pltpu.CompilerParams(collective_id=collective_id, has_side_effects=True),
-    )(x)
-
-
-def keep(total, o_ref):
-    o_ref[...] = total
-
-
-def summed(x, group, collective_id, finish=keep, rows=None):
-    block = x.shape[1:]
-    out = block if rows is None else (rows,) + block[1:]
-    kernel = functools.partial(sum_kernel, group, finish)
-    return group_call(kernel, "summed", group[0], x, block, out, collective_id)
-
-
-def spread(x, group, collective_id):
-    kernel = functools.partial(spread_kernel, group)
-    return group_call(kernel, "spread", group[0], x, x.shape, (group[0],) + x.shape, collective_id)
-
-
-def moment_rows(partials, weights, residuals):
-    values = partials.astype(jnp.float32)
-    entries = [weights * values[i] * values[j] for i, j in LOWER_PAIRS]
-    entries = entries + [weights * values[i] * residuals for i in range(5)]
-    return jnp.stack(entries)
+def stage_scratch(group, block):
+    peers = group[0] - 1
+    return [
+        pltpu.VMEM((peers,) + block, jnp.float32),
+        pltpu.SemaphoreType.DMA((peers,)),
+        pltpu.SemaphoreType.DMA((peers,)),
+    ]
 
 
 def solve_sources(moments):
@@ -171,10 +134,130 @@
     return result
 
 
-def finish_sources(total, o_ref):
+CHUNK = 1024
+LOW = 256
+ROWS = 24
+
+
+def two_parts(values):
+    high = values.astype(jnp.bfloat16)
+    return high, (values - high.astype(jnp.float32)).astype(jnp.bfloat16)
+
+
+def chosen(index, count):
+    ids = lax.broadcasted_iota(jnp.int32, (count, index.shape[1]), 0)
+    return (ids == index).astype(jnp.float32)
+
+
+def source_kernel(
+    group,
+    residuals_ref,
+    weights_ref,
+    partials_ref,
+    index_ref,
+    sources_ref,
+    new_ref,
+    weighted_ref,
+    total_ref,
+    moments,
+    solved_ref,
+    changes,
+    land_sum,
+    send_sum,
+    recv_sum,
+    land_spread,
+    send_spread,
+    recv_spread,
+):
+    count = group[0]
+    barrier = pltpu.get_barrier_semaphore()
+    peers = signal_all(barrier, group)
+    chunks = residuals_ref.shape[1] // CHUNK
+    total_ref[...] = jnp.zeros_like(total_ref)
+
+    def gather_sums(chunk, carry):
+        span = pl.ds(pl.multiple_of(chunk * CHUNK, CHUNK), CHUNK)
+        index = index_ref[:, span]
+        weights = weights_ref[:, span]
+        residuals = residuals_ref[:, span]
+        values = partials_ref[:, span].astype(jnp.float32)
+        rows = [values[i : i + 1, :] for i in range(5)]
+        scaled = [weights * row for row in rows]
+        entries = [scaled[i] * rows[j] for i, j in LOWER_PAIRS]
+        entries = entries + [scaled[i] * residuals for i in range(5)]
+        entries = entries + [jnp.zeros_like(weights)] * (ROWS - 20)
+        high, low = two_parts(jnp.concatenate(entries, axis=0))
+        both = jnp.concatenate([high, low], axis=0)
+        owner = chosen(lax.div(index, LOW), count)
+        held = [both * owner[h : h + 1, :].astype(jnp.bfloat16) for h in range(count)]
+        held = jnp.concatenate(held, axis=0)
+        picks = chosen(lax.rem(index, LOW), LOW).astype(jnp.bfloat16)
+        total_ref[...] += lax.dot_general(
+            held, picks, (((1,), (1,)), ((), ())), preferred_element_type=jnp.float32
+        )
+        return carry
+
+    lax.fori_loop(0, chunks, gather_sums, 0)
+    for h in range(count):
+        start = 2 * ROWS * h
+        moments[h] = total_ref[start : start + ROWS] + total_ref[start + ROWS : start + 2 * ROWS]
+
+    pl.semaphore_wait(barrier, peers)
+    total = sum_stage(group, moments, land_sum, send_sum, recv_sum)
     solved = solve_sources([total[r : r + 1, :] for r in range(20)])
     zero = jnp.zeros_like(solved[0])
-    o_ref[...] = jnp.concatenate(solved + [zero] * 3, axis=0)
+    solved_ref[...] = jnp.concatenate(solved + [zero] * 3, axis=0)
+
+    def place(position, block):
+        span = pl.ds(pl.multiple_of(position * LOW, LOW), LOW)
+        new_ref[:, span] = sources_ref[:, span] + block[:5]
+        changes[position] = block
+
+    spread_stage(group, solved_ref, land_spread, send_spread, recv_spread, place)
+    table = changes[...].reshape(count * 8, LOW)
+    high, low = two_parts(table)
+
+    def use_changes(chunk, carry):
+        span = pl.ds(pl.multiple_of(chunk * CHUNK, CHUNK), CHUNK)
+        index = index_ref[:, span]
+        owner = chosen(lax.div(index, LOW), count)
+        picks = chosen(lax.rem(index, LOW), LOW).astype(jnp.bfloat16)
+        found = jnp.dot(high, picks, preferred_element_type=jnp.float32)
+        found = found + jnp.dot(low, picks, preferred_element_type=jnp.float32)
+        picked = found[0:8] * owner[0:1]
+        for h in range(1, count):
+            picked = picked + found[8 * h : 8 * h + 8] * owner[h : h + 1]
+        values = partials_ref[:, span].astype(jnp.float32)
+        fitted = jnp.sum(values * picked[:5], axis=0, keepdims=True)
+        weighted_ref[:, span] = weights_ref[:, span] * (residuals_ref[:, span] - fitted)
+        return carry
+
+    lax.fori_loop(0, chunks, use_changes, 0)
+
+
+def source_updates(residuals, weights, partials, index, sources, group):
+    count = group[0]
+    return pl.pallas_call(
+        functools.partial(source_kernel, group),
+        name="source_updates",
+        out_shape=(
+            jax.ShapeDtypeStruct(sources.shape, jnp.float32),
+            jax.ShapeDtypeStruct((1,) + residuals.shape, jnp.float32),
+        ),
+        in_specs=[VMEM] * 5,
+        out_specs=(VMEM, VMEM),
+        scratch_shapes=[
+            pltpu.VMEM((count * 2 * ROWS, LOW), jnp.float32),
+            pltpu.VMEM((count, ROWS, LOW), jnp.float32),
+            pltpu.VMEM((8, LOW), jnp.float32),
+            pltpu.VMEM((count, 8, LOW), jnp.float32),
+        ]
+        + stage_scratch(group, (ROWS, LOW))
+        + stage_scratch(group, (8, LOW)),
+        compiler_params=pltpu.CompilerParams(
+            collective_id=1, has_side_effects=True, vmem_limit_bytes=48 << 20
+        ),
+    )(residuals[None], weights[None], partials, index[None], sources)
 
 
 def applied(inverse, vector, knots):
@@ -187,13 +270,46 @@
 
 
 def attitude_kernel(
-    knots, count, packed_ref, ties_ref, o_ref, inverse, sent, land, send_sem, recv_sem
+    knots,
+    count,
+    blocks_ref,
+    ties_ref,
+    o_ref,
+    inverse,
+    sent,
+    land,
+    send_sem,
+    recv_sem,
+    quarters,
+    corner,
+    eighth,
+    packed_ref,
+    *stages,
 ):
     me = lax.axis_index("tm")
+    plane, depth = along_plane(), along_depth()
     after, before = lax.rem(me + 1, count), lax.rem(me + count - 1, count)
     barrier = pltpu.get_barrier_semaphore()
     for peer in (before, after):
         pl.semaphore_signal(barrier, inc=1, device_id={"tm": peer}, device_id_type=MESH)
+    peers = 2 + signal_all(barrier, plane) + signal_all(barrier, depth)
+    pl.semaphore_wait(barrier, peers)
+
+    total = sum_stage(plane, blocks_ref, *stages[0:3])
+    for part in range(depth[0]):
+        quarters[part] = total[PIECE * part : PIECE * (part + 1)]
+    corner[...] = sum_stage(depth, quarters, *stages[3:6])
+
+    def place_quarter(position, block):
+        eighth[pl.ds(pl.multiple_of(position * PIECE, PIECE), PIECE), :] = block
+
+    spread_stage(depth, corner, *stages[6:9], place_quarter)
+    span = depth[0] * PIECE
+
+    def place_eighth(position, block):
+        packed_ref[pl.ds(pl.multiple_of(position * span, span), span), :] = block
+
+    spread_stage(plane, eighth, *stages[9:12], place_eighth)
 
     left, right = ties_ref[0:1, :], ties_ref[1:2, :]
     lanes = left.shape[1]
@@ -229,7 +345,6 @@
     base = DAMPING * applied(inverse, right_side, knots)
     lane_ids = lax.broadcasted_iota(jnp.int32, (knots, lanes), 1)
     change = base
-    pl.semaphore_wait(barrier, 2)
     for sweep in range(ITERS - 1):
         sent[sweep] = change
         copies = []
@@ -256,8 +371,10 @@
     o_ref[...] = change
 
 
-def attitude_change(packed, ties, knots, count):
+def attitude_change(blocks, ties, knots, count):
     lanes = ties.shape[1]
+    plane, depth = along_plane(), along_depth()
+    whole = (depth[0] * PIECE, lanes)
     sweeps = ITERS - 1
     return pl.pallas_call(
         functools.partial(attitude_kernel, knots, count),
@@ -271,9 +388,17 @@
             pltpu.VMEM((sweeps, 2, knots, lanes), jnp.float32),
             pltpu.SemaphoreType.DMA((sweeps, 2)),
             pltpu.SemaphoreType.DMA((sweeps, 2)),
-        ],
+            pltpu.VMEM((depth[0], PIECE, lanes), jnp.float32),
+            pltpu.VMEM((PIECE, lanes), jnp.float32),
+            pltpu.VMEM(whole, jnp.float32),
+            pltpu.VMEM((plane[0] * whole[0], lanes), jnp.float32),
+        ]
+        + stage_scratch(plane, whole)
+        + stage_scratch(depth, (PIECE, lanes))
+        + stage_scratch(depth, (PIECE, lanes))
+        + stage_scratch(plane, whole),
         compiler_params=pltpu.CompilerParams(collective_id=7, has_side_effects=True),
-    )(packed, ties)
+    )(blocks, ties)
 
 
 def on_device(
@@ -287,19 +412,14 @@
     attitude,
     coupling,
 ):
-    source_count = sources.shape[1]
     window_count, knot_count = attitude.shape
     tile_count = attitude_partials.shape[1] // TILE
     times = lax.axis_size("tm")
     time_group = along_time(times)
 
-    summands = moment_rows(source_partials, weights, residuals)
-    moments = jnp.zeros((20, source_count), jnp.float32).at[:, source_index].add(summands)
-    moments = moments.reshape(20, times, source_count // times).transpose(1, 0, 2)
-    owned = summed(moments, time_group, 1, finish_sources, 8)
-    source_change = spread(owned, time_group, 2)
-    source_change = source_change[:, :5].transpose(1, 0, 2).reshape(5, source_count)
-    new_sources = sources + source_change
+    new_sources, weighted = source_updates(
+        residuals, weights, source_partials, source_index, sources, time_group
+    )
 
     scaled = (weights[None, :] * attitude_partials.astype(jnp.float32)).astype(jnp.bfloat16)
     shaped_att = attitude_partials.reshape(knot_count, tile_count, TILE)
@@ -318,13 +438,10 @@
         axis=1,
     )
 
-    picked = source_change[:, source_index]
-    corrected = residuals - jnp.sum(source_partials.astype(jnp.float32) * picked, axis=0)
-    weighted = (weights * corrected).astype(jnp.bfloat16)
     tile_rhs = jnp.einsum(
         "ktp,tp->tk",
         shaped_att,
-        weighted.reshape(tile_count, TILE),
+        weighted.astype(jnp.bfloat16).reshape(tile_count, TILE),
         preferred_element_type=jnp.float32,
     )
     tile_rows = jnp.concatenate([tile_lower, tile_rhs], axis=1)
@@ -336,18 +453,14 @@
     )
     packed = jnp.pad(packed, ((0, 768 - packed.shape[0]), (0, 0)))
 
-    plane, depth = along_plane(), along_depth()
-    part = summed(packed.reshape(8, 96, window_count), plane, 3)
-    part = summed(part.reshape(4, 24, window_count), depth, 4)
-    part = spread(part, depth, 5).reshape(96, window_count)
-    packed = spread(part, plane, 6).reshape(768, window_count)
-
     earlier = lax.ppermute(coupling[-1:], "tm", [(i, i + 1) for i in range(times - 1)])
     left = jnp.concatenate([earlier, coupling[:-1]])
     is_final = lax.axis_index("tm") == times - 1
     final_slot = lax.broadcasted_iota(jnp.int32, (window_count,), 0) == window_count - 1
     right = jnp.where(jnp.logical_and(is_final, final_slot), 0.0, coupling)
-    change = attitude_change(packed, jnp.stack([left, right]), knot_count, times)
+    change = attitude_change(
+        packed.reshape(8, 4 * PIECE, window_count), jnp.stack([left, right]), knot_count, times
+    )
     return (new_sources, attitude + change.T)
 
 

time: 245 us -> 123 us (0.50)
  other arithmetic: 54.2 us -> 2.77 us
  local copies, waits for them, and re-layouts: 57.7 us -> 7.63 us
  Pallas kernels: 125 us -> 105 us
    pallas_call x6 -> x1, Pallas kernels: 82.2 us -> 27.7 us  [source_updates(): pl.pallas_call(functools.partial(source_kernel, group), name='source_upda...]
    scatter-add x1 -> x0, other arithmetic: 45.7 us -> none  [on_device(): jnp.zeros((20, source_count), jnp.float32).at[:, source_index].add(summands)]
    pallas_call x1, Pallas kernels: 42.7 us -> 77.5 us  [attitude_change(): pl.pallas_call(functools.partial(attitude_kernel, knots, count), name='at...]
    gather x1 -> x0, local copies, waits for them, and re-layouts: 29.3 us -> none  [on_device(): picked = source_change[:, source_index]]
    slice x1 -> x0, local copies, waits for them, and re-layouts: 9.95 us -> none  [moment_rows(): entries = [weights * values[i] * values[j] for i, j in LOWER_PAIRS]]
    another operation x2 -> x0, local copies, waits for them, and re-layouts: 5.95 us -> none  [moment_rows(): return jnp.stack(entries)]
    reshape x2 -> x0, local copies, waits for them, and re-layouts: 5.83 us -> none  [the longest x1 2.95 us: on_device(): moments.reshape(20, times, source_count // times).transpose(1, 0, 2)]
    reduce_sum x1 -> x0, other arithmetic: 3.4 us -> none  [on_device(): jnp.sum(source_partials.astype(jnp.float32) * picked, axis=0)]
  transfers between devices with their start and end apart: 1 -> 1, of which waited for: 0 -> 0; matrix products, arithmetic and copies ran while one was open for 45% -> 4% of each run, Pallas kernels for 34% -> 23%
where the time goes in v2:
time: 123 us
  Pallas kernels  105 us (85%)
  local copies, waits for them, and re-layouts  7.63 us (6%)
  starting transfers between devices  3.97 us (3%)
  other arithmetic  2.77 us (2%)
  matrix products  2.31 us (2%)
    pallas_call x1, Pallas kernels, attitude_change(): pl.pallas_call(functools.partial(attitude_kernel, knots, count), name='at...  77.5 us
    pallas_call x1, Pallas kernels, source_updates(): pl.pallas_call(functools.partial(source_kernel, group), name='source_upda...  27.7 us
    ppermute x1, starting transfers between devices, on_device(): lax.ppermute(coupling[-1:], 'tm', [(i, i + 1) for i in range(times - 1)])  3.97 us
    unnamed x25, local copies, waits for them, and re-layouts  3.71 us
  transfers between devices with their start and end apart: 1, of which 0 were waited for; matrix products, arithmetic and copies ran while one was open for 4% of the time, Pallas kernels for 23%

profile of v2, /device:TPU:4, one launch (start us, length us, event | category | flops | bytes accessed | tf_op | source)
XLA Modules:
  0.0 122.7 jit_solution(1644809054683314649)
XLA Ops:
  0.6 1.2 %slice.22 = f32[1]{0:T(128)} slice(f32[128]{0:T(128)} %param.17), slice={[127:128]} | slice | bytes 8 | tf_op jit(solution)/shard_map/slice | solution.py:456
  1.9 4.0 %collective-permute-start = (f32[1]{0:T(128)}, f32[1]{0:T(128)}, u32[]{:S(2)}, u32[]{:S(2)}) collective-permute-start(f32[1]{0:T(128)} %slice.22), channel_id=1, source_target_pairs={{0,1},{1,2},{2,3},{3,4},{4,5},{5,6},{6,7},{7,8},{8,9},{9,10},{10,1... | collective-permute-start | bytes 20 | tf_op jit(solution)/shard_map/ppermute | solution.py:456
  5.8 1.6 %fusion.4 = f32[64,32,32]{2,1,0:T(8,128)S(1)} fusion(bf16[32,8192]{1,0:T(8,128)(2,1)} %param.12, f32[8192]{0:T(1024)} %param.10), kind=kOutput, calls=%fused_computation.6 | convolution fusion | flops 17563648 | bytes 819200 | tf_op jit(solution)/shard_map/ktp,ltp->tkl/dot_general | solution.py:426
  7.4 0.3 copy.16
  7.8 0.2 fusion
  8.0 0.0 copy-start.5
  8.2 0.8 copy-done.5
  9.0 0.1 copy.17
  9.1 0.1 copy.18
  9.3 0.1 copy.19
  9.4 0.9 slice-done
  10.3 0.0 copy-start.4
  10.3 0.1 copy.20
  10.4 0.6 copy-done
  11.0 0.2 copy-done.1
  11.2 0.1 copy-done.2
  11.3 0.0 copy-done.3
  11.3 0.0 copy-done.4
  11.3 27.7 %source_updates.1 = (f32[5,4096]{1,0:T(8,128)S(1)}, f32[1,8192]{1,0:T(1,128)S(1)}) custom-call(f32[1,8192]{1,0:T(1,128)S(1)} %bitcast.46, f32[1,8192]{1,0:T(1,128)S(1)} %bitcast.45, bf16[5,8192]{1,0:T(8,128)(2,1)S(1)} %copy-done.1, s32[1,8192]{1,0:T(1,128)S(1)} %bitcast.47, f32[5,4096]{1,0:T(8,128)S(1)} %copy-done.2), custom_call_target="tpu_custom_call" | custom-call | tf_op jit(solution)/shard_map/source_updates/pallas_call | solution.py:240
  39.0 0.4 fusion.2
  39.4 0.1 copy.22
  39.5 0.7 copy-done.9
  40.2 0.0 copy-start.8
  40.2 0.6 copy-done.8
  40.9 0.4 fusion.12
  41.2 0.8 pad.4
  42.0 0.0 collective-permute-done
  42.0 0.6 maximum_bitcast_fusion
  42.6 0.6 pad_maximum_fusion.ties_ref
  43.2 77.5 %attitude_change.1 = f32[32,128]{1,0:T(8,128)} custom-call(f32[8,96,128]{2,1,0:T(8,128)} %bitcast.48, f32[2,128]{1,0:T(2,128)} %pad_maximum_fusion.ties_ref), custom_call_target="tpu_custom_call" | custom-call | tf_op jit(solution)/shard_map/attitude_change/pallas_call | solution.py:379
  120.7 1.3 %bitcast_add_fusion.1 = f32[128,32]{0,1:T(8,128)} fusion(f32[128,32]{0,1:T(8,128)S(1)} %copy-done.7, f32[32,128]{1,0:T(8,128)} %attitude_change.1), kind=kLoop, calls=%fused_computation.17 | loop fusion | flops 4096 | bytes 49152 | tf_op jit(solution)/shard_map/add | solution.py:464
  122.0 0.7 copy.42
  (20 shorter events, 0.2 us)
Async XLA Ops:
  1.9 40.1 %collective-permute-start = (f32[1]{0:T(128)}, f32[1]{0:T(128)}, u32[]{:S(2)}, u32[]{:S(2)}) collective-permute-start(f32[1]{0:T(128)} %slice.22), channel_id=1, source_target_pairs={{0,1},{1,2},{2,3},{3,4},{4,5},{5,6},{6,7},{7,8},{8,9},{9,10},{10,1... | collective-permute-start | bytes 20 | tf_op jit(solution)/shard_map/ppermute | solution.py:456
  8.0 1.0 copy-start.5
  9.0 30.0 %copy-start.6 = (bf16[32,8192]{1,0:T(8,128)(2,1)S(1)}, bf16[32,8192]{1,0:T(8,128)(2,1)}, u32[]{:S(2)}) copy-start(bf16[32,8192]{1,0:T(8,128)(2,1)} %param.12) | copy-start | bytes 1572868
  9.3 1.0 slice-start
  10.3 0.8 copy-start
  10.3 0.9 copy-start.1
  10.3 1.0 copy-start.2
  10.3 1.0 copy-start.3
  10.3 1.0 copy-start.4
  39.5 0.7 copy-start.9
  40.2 0.7 copy-start.8
  43.2 77.5 %copy-start.7 = (f32[128,32]{0,1:T(8,128)S(1)}, f32[128,32]{0,1:T(8,128)}, u32[]{:S(2)}) copy-start(f32[128,32]{0,1:T(8,128)} %param.16) | copy-start | bytes 49156

commit v3 on v2

--- a/solution.py
+++ b/solution.py
@@ -73,27 +73,47 @@
     return copies
 
 
-def sum_stage(group, x_ref, land, send_sem, recv_sem):
-    copies = send_all(group, lambda peer: x_ref.at[peer], land, send_sem, recv_sem)
+def finish_sends(copies):
+    for copy in copies:
+        copy.wait_send()
+
+
+def finish_sum(group, copies, x_ref, land):
     total = x_ref[group[1]()]
     for step, copy in enumerate(copies):
         copy.wait_recv()
         total = total + land[step]
-    for copy in copies:
-        copy.wait_send()
+    finish_sends(copies)
     return total
 
 
-def spread_stage(group, x_ref, land, send_sem, recv_sem, place):
+def finish_spread(group, copies, x_ref, land, place):
     count, spot, _ = group
     me = spot()
-    copies = send_all(group, lambda peer: x_ref, land, send_sem, recv_sem)
     place(me, x_ref[...])
     for step, copy in enumerate(copies):
         copy.wait_recv()
         place(lax.rem(me + count - step - 1, count), land[step])
-    for copy in copies:
-        copy.wait_send()
+    finish_sends(copies)
+
+
+def start_sum(group, x_ref, stage):
+    return send_all(group, lambda peer: x_ref.at[peer], *stage)
+
+
+def start_spread(group, x_ref, stage):
+    return send_all(group, lambda peer: x_ref, *stage)
+
+
+def finish_ordered(group, copies, x_ref, land, held):
+    def place(position, block):
+        held[position] = block
+
+    finish_spread(group, copies, x_ref, land, place)
+    total = held[0]
+    for position in range(1, group[0]):
+        total = total + held[position]
+    return total
 
 
 def stage_scratch(group, block):
@@ -149,29 +169,53 @@
     return (ids == index).astype(jnp.float32)
 
 
-def source_kernel(
+def applied(inverse, vector, knots):
+    parts = [None] * 4
+    for row in range(knots):
+        term = inverse[row] * vector[row : row + 1, :]
+        spot = row % 4
+        parts[spot] = term if parts[spot] is None else parts[spot] + term
+    return (parts[0] + parts[1]) + (parts[2] + parts[3])
+
+
+def update_kernel(
+    knots,
     group,
     residuals_ref,
     weights_ref,
     partials_ref,
     index_ref,
     sources_ref,
+    blocks_ref,
+    ties_ref,
+    attitude_ref,
+    window_ref,
     new_ref,
-    weighted_ref,
+    o_ref,
     total_ref,
     moments,
     solved_ref,
     changes,
-    land_sum,
-    send_sum,
-    recv_sum,
-    land_spread,
-    send_spread,
-    recv_spread,
+    quarters,
+    corner,
+    eighth,
+    packed_ref,
+    rhs_ref,
+    rhs_part,
+    rhs_plane,
+    rhs_depth,
+    inverse,
+    sent,
+    land,
+    send_sem,
+    recv_sem,
+    *scratch,
 ):
+    stages = [scratch[i : i + 3] for i in range(0, len(scratch), 3)]
+    plane, depth = along_plane(), along_depth()
     count = group[0]
     barrier = pltpu.get_barrier_semaphore()
-    peers = signal_all(barrier, group)
+    peers = signal_all(barrier, group) + signal_all(barrier, plane) + signal_all(barrier, depth)
     chunks = residuals_ref.shape[1] // CHUNK
     total_ref[...] = jnp.zeros_like(total_ref)
 
@@ -203,17 +247,29 @@
         moments[h] = total_ref[start : start + ROWS] + total_ref[start + ROWS : start + 2 * ROWS]
 
     pl.semaphore_wait(barrier, peers)
-    total = sum_stage(group, moments, land_sum, send_sum, recv_sum)
+    plane_sum = start_sum(plane, blocks_ref, stages[2])
+    time_sum = start_sum(group, moments, stages[0])
+
+    total = finish_sum(plane, plane_sum, blocks_ref, stages[2][0])
+    for part in range(depth[0]):
+        quarters[part] = total[PIECE * part : PIECE * (part + 1)]
+    depth_sum = start_sum(depth, quarters, stages[3])
+
+    total = finish_sum(group, time_sum, moments, stages[0][0])
     solved = solve_sources([total[r : r + 1, :] for r in range(20)])
     zero = jnp.zeros_like(solved[0])
     solved_ref[...] = jnp.concatenate(solved + [zero] * 3, axis=0)
+    time_spread = start_spread(group, solved_ref, stages[1])
+
+    corner[...] = finish_sum(depth, depth_sum, quarters, stages[3][0])
+    depth_spread = start_spread(depth, corner, stages[4])
 
     def place(position, block):
         span = pl.ds(pl.multiple_of(position * LOW, LOW), LOW)
         new_ref[:, span] = sources_ref[:, span] + block[:5]
         changes[position] = block
 
-    spread_stage(group, solved_ref, land_spread, send_spread, recv_spread, place)
+    finish_spread(group, time_spread, solved_ref, stages[1][0], place)
     table = changes[...].reshape(count * 8, LOW)
     high, low = two_parts(table)
 
@@ -229,90 +285,36 @@
             picked = picked + found[8 * h : 8 * h + 8] * owner[h : h + 1]
         values = partials_ref[:, span].astype(jnp.float32)
         fitted = jnp.sum(values * picked[:5], axis=0, keepdims=True)
-        weighted_ref[:, span] = weights_ref[:, span] * (residuals_ref[:, span] - fitted)
+        weighted = weights_ref[:, span] * (residuals_ref[:, span] - fitted)
+        tied = chosen(window_ref[:, span], lanes) * weighted.astype(jnp.bfloat16).astype(jnp.float32)
+        rhs_ref[...] += lax.dot_general(
+            attitude_ref[:, span],
+            tied.astype(jnp.bfloat16),
+            (((1,), (1,)), ((), ())),
+            preferred_element_type=jnp.float32,
+        )
         return carry
 
+    lanes = ties_ref.shape[1]
+    rhs_ref[...] = jnp.zeros_like(rhs_ref)
     lax.fori_loop(0, chunks, use_changes, 0)
-
-
-def source_updates(residuals, weights, partials, index, sources, group):
-    count = group[0]
-    return pl.pallas_call(
-        functools.partial(source_kernel, group),
-        name="source_updates",
-        out_shape=(
-            jax.ShapeDtypeStruct(sources.shape, jnp.float32),
-            jax.ShapeDtypeStruct((1,) + residuals.shape, jnp.float32),
-        ),
-        in_specs=[VMEM] * 5,
-        out_specs=(VMEM, VMEM),
-        scratch_shapes=[
-            pltpu.VMEM((count * 2 * ROWS, LOW), jnp.float32),
-            pltpu.VMEM((count, ROWS, LOW), jnp.float32),
-            pltpu.VMEM((8, LOW), jnp.float32),
-            pltpu.VMEM((count, 8, LOW), jnp.float32),
-        ]
-        + stage_scratch(group, (ROWS, LOW))
-        + stage_scratch(group, (8, LOW)),
-        compiler_params=pltpu.CompilerParams(
-            collective_id=1, has_side_effects=True, vmem_limit_bytes=48 << 20
-        ),
-    )(residuals[None], weights[None], partials, index[None], sources)
-
-
-def applied(inverse, vector, knots):
-    parts = [None] * 4
-    for row in range(knots):
-        term = inverse[row] * vector[row : row + 1, :]
-        spot = row % 4
-        parts[spot] = term if parts[spot] is None else parts[spot] + term
-    return (parts[0] + parts[1]) + (parts[2] + parts[3])
-
-
-def attitude_kernel(
-    knots,
-    count,
-    blocks_ref,
-    ties_ref,
-    o_ref,
-    inverse,
-    sent,
-    land,
-    send_sem,
-    recv_sem,
-    quarters,
-    corner,
-    eighth,
-    packed_ref,
-    *stages,
-):
-    me = lax.axis_index("tm")
-    plane, depth = along_plane(), along_depth()
-    after, before = lax.rem(me + 1, count), lax.rem(me + count - 1, count)
-    barrier = pltpu.get_barrier_semaphore()
-    for peer in (before, after):
-        pl.semaphore_signal(barrier, inc=1, device_id={"tm": peer}, device_id_type=MESH)
-    peers = 2 + signal_all(barrier, plane) + signal_all(barrier, depth)
-    pl.semaphore_wait(barrier, peers)
-
-    total = sum_stage(plane, blocks_ref, *stages[0:3])
-    for part in range(depth[0]):
-        quarters[part] = total[PIECE * part : PIECE * (part + 1)]
-    corner[...] = sum_stage(depth, quarters, *stages[3:6])
+    rhs_first = start_spread(plane, rhs_ref, stages[6])
 
     def place_quarter(position, block):
         eighth[pl.ds(pl.multiple_of(position * PIECE, PIECE), PIECE), :] = block
 
-    spread_stage(depth, corner, *stages[6:9], place_quarter)
-    span = depth[0] * PIECE
+    finish_spread(depth, depth_spread, corner, stages[4][0], place_quarter)
+    plane_spread = start_spread(plane, eighth, stages[5])
+    rhs_part[...] = finish_ordered(plane, rhs_first, rhs_ref, stages[6][0], rhs_plane)
+    rhs_second = start_spread(depth, rhs_part, stages[7])
+    width = depth[0] * PIECE
 
     def place_eighth(position, block):
-        packed_ref[pl.ds(pl.multiple_of(position * span, span), span), :] = block
-
-    spread_stage(plane, eighth, *stages[9:12], place_eighth)
+        packed_ref[pl.ds(pl.multiple_of(position * width, width), width), :] = block
+
+    finish_spread(plane, plane_spread, eighth, stages[5][0], place_eighth)
 
     left, right = ties_ref[0:1, :], ties_ref[1:2, :]
-    lanes = left.shape[1]
     row_ids = lax.broadcasted_iota(jnp.int32, (knots, lanes), 0)
     start = 0
     for group in range(knots // BLOCK):
@@ -327,29 +329,32 @@
             rows = pl.ds(high * BLOCK, BLOCK)
             for k in range(low * BLOCK, (low + 1) * BLOCK):
                 inverse[k, rows, :] = inverse[rows, k, :]
-    right_side = packed_ref[start : start + knots, :]
 
     def pivot(p, carry):
         own = inverse[p]
         here = row_ids == p
         scale = 1.0 / inverse[p, pl.ds(p, 1), :]
         row = jnp.where(here, scale, own * scale)
+        factors = jnp.where(row_ids < p, -own, own)
         for i in range(knots):
-            factor = inverse[i, pl.ds(p, 1), :]
-            inverse[i] = jnp.where(here, 0.0, inverse[i]) - factor * row
+            inverse[i] = jnp.where(here, 0.0, inverse[i]) - factors[i : i + 1, :] * row
         inverse[p] = row
         return carry
 
     lax.fori_loop(0, knots, pivot, 0)
 
+    right_side = finish_ordered(depth, rhs_second, rhs_part, stages[7][0], rhs_depth)
     base = DAMPING * applied(inverse, right_side, knots)
     lane_ids = lax.broadcasted_iota(jnp.int32, (knots, lanes), 1)
+    first, last = lane_ids == 0, lane_ids == lanes - 1
+    me = lax.axis_index("tm")
+    has_before, has_after = me > 0, me < count - 1
+    after, before = lax.rem(me + 1, count), lax.rem(me + count - 1, count)
     change = base
     for sweep in range(ITERS - 1):
         sent[sweep] = change
-        copies = []
-        for side, peer in enumerate((after, before)):
-            copy = pltpu.make_async_remote_copy(
+        ahead, behind = [
+            pltpu.make_async_remote_copy(
                 src_ref=sent.at[sweep],
                 dst_ref=land.at[sweep, side],
                 send_sem=send_sem.at[sweep, side],
@@ -357,48 +362,73 @@
                 device_id={"tm": peer},
                 device_id_type=MESH,
             )
-            copy.start()
-            copies.append(copy)
-        own_low, own_high = pltpu.roll(change, 1, 1), pltpu.roll(change, lanes - 1, 1)
-        for copy in copies:
-            copy.wait()
-        low = jnp.where(lane_ids == 0, pltpu.roll(land[sweep, 0], 1, 1), own_low)
-        high = jnp.where(
-            lane_ids == lanes - 1, pltpu.roll(land[sweep, 1], lanes - 1, 1), own_high
-        )
+            for side, peer in enumerate((after, before))
+        ]
+        pl.when(has_after)(ahead.start)
+        pl.when(has_before)(behind.start)
+        own_low = jnp.where(first, 0.0, pltpu.roll(change, 1, 1))
+        own_high = jnp.where(last, 0.0, pltpu.roll(change, lanes - 1, 1))
+        pl.when(has_before)(ahead.wait_recv)
+        pl.when(has_after)(behind.wait_recv)
+        low, high = pltpu.roll(land[sweep, 0], 1, 1), pltpu.roll(land[sweep, 1], lanes - 1, 1)
+        low = jnp.where(jnp.logical_and(first, has_before), low, own_low)
+        high = jnp.where(jnp.logical_and(last, has_after), high, own_high)
         tied = left * low + right * high
         change = (1.0 - DAMPING) * change + base + DAMPING * applied(inverse, tied, knots)
+        pl.when(has_after)(ahead.wait_send)
+        pl.when(has_before)(behind.wait_send)
     o_ref[...] = change
 
 
-def attitude_change(blocks, ties, knots, count):
-    lanes = ties.shape[1]
+def updates(residuals, weights, partials, index, sources, blocks, ties, attitude, window, group):
+    knots, lanes, count = attitude.shape[0], ties.shape[1], group[0]
+    sweeps = ITERS - 1
     plane, depth = along_plane(), along_depth()
-    whole = (depth[0] * PIECE, lanes)
-    sweeps = ITERS - 1
+    piece, whole, side = (PIECE, lanes), (depth[0] * PIECE, lanes), (knots, lanes)
+
+    def held(*shape):
+        return pltpu.VMEM(shape, jnp.float32)
+
     return pl.pallas_call(
-        functools.partial(attitude_kernel, knots, count),
-        name="attitude_change",
-        out_shape=jax.ShapeDtypeStruct((knots, lanes), jnp.float32),
-        in_specs=[VMEM, VMEM],
-        out_specs=VMEM,
+        functools.partial(update_kernel, knots, group),
+        name="updates",
+        out_shape=(
+            jax.ShapeDtypeStruct(sources.shape, jnp.float32),
+            jax.ShapeDtypeStruct(side, jnp.float32),
+        ),
+        in_specs=[VMEM] * 9,
+        out_specs=(VMEM, VMEM),
         scratch_shapes=[
-            pltpu.VMEM((knots, knots, lanes), jnp.float32),
-            pltpu.VMEM((sweeps, knots, lanes), jnp.float32),
-            pltpu.VMEM((sweeps, 2, knots, lanes), jnp.float32),
+            held(count * 2 * ROWS, LOW),
+            held(count, ROWS, LOW),
+            held(8, LOW),
+            held(count, 8, LOW),
+            held(depth[0], *piece),
+            held(*piece),
+            held(*whole),
+            held(plane[0] * whole[0], lanes),
+            held(*side),
+            held(*side),
+            held(plane[0], *side),
+            held(depth[0], *side),
+            held(knots, *side),
+            held(sweeps, *side),
+            held(sweeps, 2, *side),
             pltpu.SemaphoreType.DMA((sweeps, 2)),
             pltpu.SemaphoreType.DMA((sweeps, 2)),
-            pltpu.VMEM((depth[0], PIECE, lanes), jnp.float32),
-            pltpu.VMEM((PIECE, lanes), jnp.float32),
-            pltpu.VMEM(whole, jnp.float32),
-            pltpu.VMEM((plane[0] * whole[0], lanes), jnp.float32),
         ]
+        + stage_scratch(group, (ROWS, LOW))
+        + stage_scratch(group, (8, LOW))
         + stage_scratch(plane, whole)
-        + stage_scratch(depth, (PIECE, lanes))
-        + stage_scratch(depth, (PIECE, lanes))
-        + stage_scratch(plane, whole),
-        compiler_params=pltpu.CompilerParams(collective_id=7, has_side_effects=True),
-    )(blocks, ties)
+        + stage_scratch(depth, piece)
+        + stage_scratch(depth, piece)
+        + stage_scratch(plane, whole)
+        + stage_scratch(plane, side)
+        + stage_scratch(depth, side),
+        compiler_params=pltpu.CompilerParams(
+            collective_id=1, has_side_effects=True, vmem_limit_bytes=48 << 20
+        ),
+    )(residuals[None], weights[None], partials, index[None], sources, blocks, ties, attitude, window[None])
 
 
 def on_device(
@@ -416,10 +446,6 @@
     tile_count = attitude_partials.shape[1] // TILE
     times = lax.axis_size("tm")
     time_group = along_time(times)
-
-    new_sources, weighted = source_updates(
-        residuals, weights, source_partials, source_index, sources, time_group
-    )
 
     scaled = (weights[None, :] * attitude_partials.astype(jnp.float32)).astype(jnp.bfloat16)
     shaped_att = attitude_partials.reshape(knot_count, tile_count, TILE)
@@ -438,18 +464,11 @@
         axis=1,
     )
 
-    tile_rhs = jnp.einsum(
-        "ktp,tp->tk",
-        shaped_att,
-        weighted.astype(jnp.bfloat16).reshape(tile_count, TILE),
-        preferred_element_type=jnp.float32,
-    )
-    tile_rows = jnp.concatenate([tile_lower, tile_rhs], axis=1)
     first_window = lax.axis_index("tm") * window_count
     window_ids = lax.broadcasted_iota(jnp.int32, (tile_count, window_count), 1)
     selector = (tile_window[:, None] - first_window == window_ids).astype(jnp.float32)
     packed = lax.dot_general(
-        tile_rows, selector, (((0,), (0,)), ((), ())), precision=HIGHEST
+        tile_lower, selector, (((0,), (0,)), ((), ())), precision=HIGHEST
     )
     packed = jnp.pad(packed, ((0, 768 - packed.shape[0]), (0, 0)))
 
@@ -458,8 +477,17 @@
     is_final = lax.axis_index("tm") == times - 1
     final_slot = lax.broadcasted_iota(jnp.int32, (window_count,), 0) == window_count - 1
     right = jnp.where(jnp.logical_and(is_final, final_slot), 0.0, coupling)
-    change = attitude_change(
-        packed.reshape(8, 4 * PIECE, window_count), jnp.stack([left, right]), knot_count, times
+    new_sources, change = updates(
+        residuals,
+        weights,
+        source_partials,
+        source_index,
+        sources,
+        packed.reshape(8, 4 * PIECE, window_count),
+        jnp.stack([left, right]),
+        attitude_partials,
+        jnp.repeat(tile_window - first_window, TILE, total_repeat_length=residuals.shape[0]),
+        time_group,
     )
     return (new_sources, attitude + change.T)
 

time: 123 us -> 144 us (1.17)
  the two profiles are of different devices: /device:TPU:4 before, /device:TPU:24 now
where the time goes in v3:
time: 144 us; the launch traced here: 143 us
  Pallas kernels  81.7 us (57%)
  other arithmetic  48 us (33%)
  local copies, waits for them, and re-layouts  7.16 us (5%)
  starting transfers between devices  3.47 us (2%)
  matrix products  2.06 us (1%)
    pallas_call x1, Pallas kernels, updates(): pl.pallas_call(functools.partial(update_kernel, knots, group), name='upda...  81.7 us
    gather x3, other arithmetic, on_device(): jnp.repeat(tile_window - first_window, TILE, total_repeat_length=residual...  46.3 us
    ppermute x1, starting transfers between devices, on_device(): lax.ppermute(coupling[-1:], 'tm', [(i, i + 1) for i in range(times - 1)])  3.47 us
  transfers between devices with their start and end apart: 1, of which 0 were waited for; matrix products, arithmetic and copies ran while one was open for 37% of the time, Pallas kernels for 0%

profile of v3, /device:TPU:24, one launch (start us, length us, event | category | flops | bytes accessed | tf_op | source)
XLA Modules:
  0.0 143.3 jit_solution(8965116388606255987)
XLA Ops:
  0.6 1.2 slice.38
  1.9 3.5 %collective-permute-start = (f32[1]{0:T(128)}, f32[1]{0:T(128)}, u32[]{:S(2)}, u32[]{:S(2)}) collective-permute-start(f32[1]{0:T(128)} %slice.38), channel_id=1, source_target_pairs={{0,1},{1,2},{2,3},{3,4},{4,5},{5,6},{6,7},{7,8},{8,9},{9,10},{10,1... | collective-permute-start | bytes 20 | tf_op jit(solution)/shard_map/ppermute | solution.py:475
  5.3 1.7 %fusion.2 = f32[64,32,32]{2,1,0:T(8,128)S(1)} fusion(bf16[32,8192]{1,0:T(8,128)(2,1)} %attitude_ref.1, f32[8192]{0:T(1024)} %param.12), kind=kOutput, calls=%fused_computation.4 | convolution fusion | flops 17563648 | bytes 819200 | tf_op jit(solution)/shard_map/ktp,ltp->tkl/dot_general | solution.py:452
  7.1 0.3 copy.16
  7.4 0.2 fusion
  7.8 0.0 copy-start.7
  7.8 0.6 copy-done.7
  8.5 0.7 fusion.22
  9.2 0.7 fusion.23
  9.9 0.7 fusion.20
  10.6 0.7 fusion.21
  11.4 0.1 copy.20
  11.5 0.1 copy.19
  11.6 0.1 copy.18
  11.8 0.1 copy.17
  11.9 0.7 copy-done.8
  12.6 4.4 %compare_select_fusion.2 = (s32[8192,1]{0,1:T(1,128)S(1)}, s32[8192,1]{0,1:T(1,128)S(1)}) fusion(s32[]{:T(128)} %bitcast.72, s32[]{:T(128)} %bitcast.73, s32[]{:T(128)} %bitcast.74, s32[]{:T(128)} %bitcast.75, s32[]{:T(128)} %bitcast.76, s32[]{:T(128)} %bitcast.78, s32[]{:T(128)} %bitcast.77, s32[8192,1]{0,1:T(1,128)S(1)} %bitcast.109, ...), kind=kLoop, calls=%fused_computation.76 | loop fusion | flops 114688 | bytes 131100 | tf_op jit(solution)/shard_map/jit(_take)/gather | solution.py:489
  17.0 5.8 %compare_reduce_fusion.56 = (pred[8192]{0:T(1024)(128)(4,1)S(1)}, pred[8192]{0:T(1024)(128)(4,1)S(1)}, pred[8192]{0:T(1024)(128)(4,1)S(1)}, pred[8192]{0:T(1024)...) fusion(s32[8192,1]{0,1:T(1,128)S(1)} %get-tuple-element.76), kind=kLoop, calls=%fused_computation.75 | loop fusion | flops 466944 | bytes 499712 | tf_op jit(solution)/shard_map/jit(_take)/gather | solution.py:489
  22.8 0.3 fusion.7
  23.2 0.0 copy-start
  23.2 0.0 copy-start.2
  23.2 0.0 copy-start.3
  23.3 36.1 %select_select_fusion = s32[8192]{0:T(1024)S(1)} fusion(pred[8192]{0:T(1024)(128)(4,1)S(1)} %get-tuple-element.74, pred[8192]{0:T(1024)(128)(4,1)S(1)} %get-tuple-element.73, pred[8192]{0:T(1024)(128)(4,1)S(1)} %get-tuple-element.72, pred[8192]{0:T(1024)(128)(4,1)S(1)} %get-tuple-element.71, pred[8192]{0:T(1024)(128)(4,1)S(1)} %get-tuple-element.70, ...), kind=kLoop, calls=%fused_computation.83 | loop fusion | flops 466944 | bytes 532708 | tf_op jit(solution)/shard_map/jit(_take)/gather | solution.py:489
  59.3 0.0 copy-start.1
  59.3 0.0 copy-start.4
  59.4 0.0 copy-start.5
  59.4 0.1 and_select_fusion.window_ref
  59.5 0.8 maximum_bitcast_fusion
  60.3 0.0 copy-start.6
  60.3 81.7 %updates.1 = (f32[5,4096]{1,0:T(8,128)S(1)}, f32[32,128]{1,0:T(8,128)S(1)}) custom-call(f32[1,8192]{1,0:T(1,128)S(1)} %bitcast.105, f32[1,8192]{1,0:T(1,128)S(1)} %bitcast.104, bf16[5,8192]{1,0:T(8,128)(2,1)S(1)} %copy-done.2, s32[1,8192]{1,0:T(1,128)S(1)} %bitcast.106, f32[5,4096]{1,0:T(8,128)S(1)} %copy-done.3, f32[8,96,128]{2,1,0:T(8,128)S(1)} %bitcast.103, ...), custom_call_target="tpu_custom_call" | custom-call | tf_op jit(solution)/shard_map/updates/pallas_call | solution.py:392
  142.0 0.6 bitcast_add_fusion.1
  142.6 0.7 copy.32
  (19 shorter events, 0.2 us)
Async XLA Ops:
  1.9 57.6 %collective-permute-start = (f32[1]{0:T(128)}, f32[1]{0:T(128)}, u32[]{:S(2)}, u32[]{:S(2)}) collective-permute-start(f32[1]{0:T(128)} %slice.38), channel_id=1, source_target_pairs={{0,1},{1,2},{2,3},{3,4},{4,5},{5,6},{6,7},{7,8},{8,9},{9,10},{10,1... | collective-permute-start | bytes 20 | tf_op jit(solution)/shard_map/ppermute | solution.py:475
  7.8 0.7 copy-start.7
  11.9 0.7 copy-start.8
  23.2 37.0 %copy-start = (bf16[32,8192]{1,0:T(8,128)(2,1)S(1)}, bf16[32,8192]{1,0:T(8,128)(2,1)}, u32[]{:S(2)}) copy-start(bf16[32,8192]{1,0:T(8,128)(2,1)} %attitude_ref.1) | copy-start | bytes 1572868
  23.2 37.0 %copy-start.2 = (bf16[5,8192]{1,0:T(8,128)(2,1)S(1)}, bf16[5,8192]{1,0:T(8,128)(2,1)}, u32[]{:S(2)}) copy-start(bf16[5,8192]{1,0:T(8,128)(2,1)} %partials_ref.1) | copy-start | bytes 245764
  23.2 37.0 %copy-start.3 = (f32[5,4096]{1,0:T(8,128)S(1)}, f32[5,4096]{1,0:T(8,128)}, u32[]{:S(2)}) copy-start(f32[5,4096]{1,0:T(8,128)} %sources_ref.1) | copy-start | bytes 245764
  59.3 0.9 copy-start.1
  59.3 0.9 copy-start.4
  59.4 0.9 copy-start.5
  60.3 81.7 %copy-start.6 = (f32[128,32]{0,1:T(8,128)S(1)}, f32[128,32]{0,1:T(8,128)}, u32[]{:S(2)}) copy-start(f32[128,32]{0,1:T(8,128)} %param.18) | copy-start | bytes 49156

commit v4 on v3

--- a/solution.py
+++ b/solution.py
@@ -486,7 +486,7 @@
         packed.reshape(8, 4 * PIECE, window_count),
         jnp.stack([left, right]),
         attitude_partials,
-        jnp.repeat(tile_window - first_window, TILE, total_repeat_length=residuals.shape[0]),
+        jnp.broadcast_to((tile_window - first_window)[:, None], (tile_count, TILE)).reshape(-1),
         time_group,
     )
     return (new_sources, attitude + change.T)

time: 144 us -> 94.1 us (0.65)
  other arithmetic: 48 us -> 1.61 us
  local copies, waits for them, and re-layouts: 7.16 us -> 4.51 us
    gather x3 -> x0, other arithmetic: 46.3 us -> none  [on_device(): jnp.repeat(tile_window - first_window, TILE, total_repeat_length=residual...]
    gather x4 -> x0, local copies, waits for them, and re-layouts: 2.84 us -> none  [on_device(): jnp.repeat(tile_window - first_window, TILE, total_repeat_length=residual...]
  transfers between devices with their start and end apart: 1 -> 1, of which waited for: 0 -> 0; matrix products, arithmetic and copies ran while one was open for 37% -> 3% of each run, Pallas kernels for 0% -> 0%
where the time goes in v4:
time: 94.1 us; the launch traced here: 93.8 us
  Pallas kernels  81.5 us (87%)
  local copies, waits for them, and re-layouts  4.51 us (5%)
  starting transfers between devices  3.47 us (4%)
  matrix products  1.96 us (2%)
  other arithmetic  1.61 us (2%)
    pallas_call x1, Pallas kernels, updates(): pl.pallas_call(functools.partial(update_kernel, knots, group), name='upda...  81.5 us
    ppermute x1, starting transfers between devices, on_device(): lax.ppermute(coupling[-1:], 'tm', [(i, i + 1) for i in range(times - 1)])  3.47 us
    unnamed x19, local copies, waits for them, and re-layouts  2.15 us
  transfers between devices with their start and end apart: 1, of which 0 were waited for; matrix products, arithmetic and copies ran while one was open for 3% of the time, Pallas kernels for 0%

profile of v4, /device:TPU:24, one launch (start us, length us, event | category | flops | bytes accessed | tf_op | source)
XLA Modules:
  0.0 93.8 jit_solution(10316164991180401709)
XLA Ops:
  0.6 1.2 %slice.22 = f32[1]{0:T(128)} slice(f32[128]{0:T(128)} %param.17), slice={[127:128]} | slice | bytes 8 | tf_op jit(solution)/shard_map/slice | solution.py:475
  1.9 3.5 %collective-permute-start = (f32[1]{0:T(128)}, f32[1]{0:T(128)}, u32[]{:S(2)}, u32[]{:S(2)}) collective-permute-start(f32[1]{0:T(128)} %slice.22), channel_id=1, source_target_pairs={{0,1},{1,2},{2,3},{3,4},{4,5},{5,6},{6,7},{7,8},{8,9},{9,10},{10,1... | collective-permute-start | bytes 20 | tf_op jit(solution)/shard_map/ppermute | solution.py:475
  5.3 1.6 %fusion.2 = f32[64,32,32]{2,1,0:T(8,128)S(1)} fusion(bf16[32,8192]{1,0:T(8,128)(2,1)} %attitude_ref.1, f32[8192]{0:T(1024)} %param.10), kind=kOutput, calls=%fused_computation.4 | convolution fusion | flops 17563648 | bytes 819200 | tf_op jit(solution)/shard_map/ktp,ltp->tkl/dot_general | solution.py:452
  7.0 0.3 copy.16
  7.3 0.2 fusion
  7.7 0.1 copy.20
  7.8 0.1 copy.19
  8.0 0.1 copy.18
  8.1 0.1 copy.17
  8.3 0.7 copy-done.8
  8.9 0.0 copy-start.7
  8.9 0.6 copy-done.7
  9.6 0.0 copy-start.3
  9.6 0.4 fusion.7
  10.0 0.0 copy-start
  10.0 0.0 copy-start.2
  10.0 0.0 copy-start.4
  10.0 0.0 copy-start.5
  10.0 0.0 copy-start.1
  10.1 0.0 collective-permute-done
  10.1 0.8 maximum_bitcast_fusion
  10.8 0.1 eq.17
  10.9 0.0 copy-done.3
  10.9 0.1 copy-done
  11.0 0.0 copy-done.2
  11.0 0.0 copy-done.4
  11.0 0.0 copy-done.5
  11.0 0.0 copy-done.1
  11.1 81.5 %updates.1 = (f32[5,4096]{1,0:T(8,128)S(1)}, f32[32,128]{1,0:T(8,128)S(1)}) custom-call(f32[1,8192]{1,0:T(1,128)S(1)} %bitcast.37, f32[1,8192]{1,0:T(1,128)S(1)} %bitcast.35, bf16[5,8192]{1,0:T(8,128)(2,1)S(1)} %copy-done.2, s32[1,8192]{1,0:T(1,128)S(1)} %bitcast.38, f32[5,4096]{1,0:T(8,128)S(1)} %copy-done.3, f32[8,96,128]{2,1,0:T(8,128)S(1)} %bitcast.34, ...), custom_call_target="tpu_custom_call" | custom-call | tf_op jit(solution)/shard_map/updates/pallas_call | solution.py:392
  92.6 0.0 copy-done.6
  92.6 0.6 bitcast_add_fusion.1
  93.2 0.7 copy.32
  (10 shorter events, 0.2 us)
Async XLA Ops:
  1.9 8.2 %collective-permute-start = (f32[1]{0:T(128)}, f32[1]{0:T(128)}, u32[]{:S(2)}, u32[]{:S(2)}) collective-permute-start(f32[1]{0:T(128)} %slice.22), channel_id=1, source_target_pairs={{0,1},{1,2},{2,3},{3,4},{4,5},{5,6},{6,7},{7,8},{8,9},{9,10},{10,1... | collective-permute-start | bytes 20 | tf_op jit(solution)/shard_map/ppermute | solution.py:475
  8.3 0.7 copy-start.8
  8.9 0.7 copy-start.7
  9.6 1.3 %copy-start.3 = (f32[5,4096]{1,0:T(8,128)S(1)}, f32[5,4096]{1,0:T(8,128)}, u32[]{:S(2)}) copy-start(f32[5,4096]{1,0:T(8,128)} %sources_ref.1) | copy-start | bytes 245764
  10.0 1.1 %copy-start = (bf16[32,8192]{1,0:T(8,128)(2,1)S(1)}, bf16[32,8192]{1,0:T(8,128)(2,1)}, u32[]{:S(2)}) copy-start(bf16[32,8192]{1,0:T(8,128)(2,1)} %attitude_ref.1) | copy-start | bytes 1572868
  10.0 1.1 %copy-start.2 = (bf16[5,8192]{1,0:T(8,128)(2,1)S(1)}, bf16[5,8192]{1,0:T(8,128)(2,1)}, u32[]{:S(2)}) copy-start(bf16[5,8192]{1,0:T(8,128)(2,1)} %partials_ref.1) | copy-start | bytes 245764
  10.0 1.1 %copy-start.4 = (f32[8192]{0:T(1024)S(1)}, f32[8192]{0:T(1024)}, u32[]{:S(2)}) copy-start(f32[8192]{0:T(1024)} %param.9) | copy-start | bytes 98308
  10.0 1.1 %copy-start.5 = (s32[8192]{0:T(1024)S(1)}, s32[8192]{0:T(1024)}, u32[]{:S(2)}) copy-start(s32[8192]{0:T(1024)} %param.13) | copy-start | bytes 98308
  10.0 1.0 %copy-start.1 = (f32[8192]{0:T(1024)S(1)}, f32[8192]{0:T(1024)}, u32[]{:S(2)}) copy-start(f32[8192]{0:T(1024)} %param.10) | copy-start | bytes 98308
  11.1 81.5 %copy-start.6 = (f32[128,32]{0,1:T(8,128)S(1)}, f32[128,32]{0,1:T(8,128)}, u32[]{:S(2)}) copy-start(f32[128,32]{0,1:T(8,128)} %param.16) | copy-start | bytes 49156

commit v5 on v4

--- a/solution.py
+++ b/solution.py
@@ -116,12 +116,60 @@
     return total
 
 
+def neighbours(source, land, send_sem, recv_sem, count):
+    me = lax.axis_index("tm")
+    after, before = lax.rem(me + 1, count), lax.rem(me + count - 1, count)
+    return [
+        pltpu.make_async_remote_copy(
+            src_ref=source,
+            dst_ref=land.at[side],
+            send_sem=send_sem.at[side],
+            recv_sem=recv_sem.at[side],
+            device_id={"tm": peer},
+            device_id_type=MESH,
+        )
+        for side, peer in enumerate((after, before))
+    ]
+
+
+def start_sides(source, stage, count):
+    me = lax.axis_index("tm")
+    ahead, behind = neighbours(source, *stage, count)
+    pl.when(me < count - 1)(ahead.start)
+    pl.when(me > 0)(behind.start)
+    return ahead, behind
+
+
+def finish_sides(copies, source, land, count):
+    me = lax.axis_index("tm")
+    has_before, has_after = me > 0, me < count - 1
+    ahead, behind = copies
+    pl.when(has_before)(ahead.wait_recv)
+    pl.when(has_after)(behind.wait_recv)
+    pl.when(has_after)(ahead.wait_send)
+    pl.when(has_before)(behind.wait_send)
+    own = source[...]
+    lanes = lax.broadcasted_iota(jnp.int32, own.shape, 1)
+    half = own.shape[1] // 2
+    halo = jnp.where(jnp.logical_and(lanes < half, has_after), land[1], own)
+    halo = jnp.where(jnp.logical_and(lanes >= half, has_before), land[0], halo)
+    return jnp.concatenate([own, halo], axis=1)
+
+
 def stage_scratch(group, block):
     peers = group[0] - 1
     return [
         pltpu.VMEM((peers,) + block, jnp.float32),
         pltpu.SemaphoreType.DMA((peers,)),
         pltpu.SemaphoreType.DMA((peers,)),
+    ]
+
+
+def side_scratch(block):
+    return [
+        pltpu.VMEM((2,) + block, jnp.float32),
+        pltpu.SemaphoreType.DMA((2,)),
+        pltpu.SemaphoreType.DMA((2,)),
     ]
 
 
@@ -205,10 +253,8 @@
     rhs_plane,
     rhs_depth,
     inverse,
-    sent,
-    land,
-    send_sem,
-    recv_sem,
+    wide_corner,
+    rhs_total,
     *scratch,
 ):
     stages = [scratch[i : i + 3] for i in range(0, len(scratch), 3)]
@@ -261,8 +307,9 @@
     solved_ref[...] = jnp.concatenate(solved + [zero] * 3, axis=0)
     time_spread = start_spread(group, solved_ref, stages[1])
 
-    corner[...] = finish_sum(depth, depth_sum, quarters, stages[3][0])
-    depth_spread = start_spread(depth, corner, stages[4])
+    corner[:PIECE, :] = finish_sum(depth, depth_sum, quarters, stages[3][0])
+    corner[PIECE:, :] = jnp.concatenate([ties_ref[...]] + [jnp.zeros_like(ties_ref[...])] * 3, axis=0)
+    corner_sides = start_sides(corner, stages[8], count)
 
     def place(position, block):
         span = pl.ds(pl.multiple_of(position * LOW, LOW), LOW)
@@ -270,6 +317,10 @@
         changes[position] = block
 
     finish_spread(group, time_spread, solved_ref, stages[1][0], place)
+    wide = finish_sides(corner_sides, corner, stages[8][0], count)
+    wide_corner[...] = wide[:PIECE]
+    depth_spread = start_spread(depth, wide_corner, stages[4])
+    left, right = wide[PIECE : PIECE + 1], wide[PIECE + 1 : PIECE + 2]
     table = changes[...].reshape(count * 8, LOW)
     high, low = two_parts(table)
 
@@ -303,7 +354,7 @@
     def place_quarter(position, block):
         eighth[pl.ds(pl.multiple_of(position * PIECE, PIECE), PIECE), :] = block
 
-    finish_spread(depth, depth_spread, corner, stages[4][0], place_quarter)
+    finish_spread(depth, depth_spread, wide_corner, stages[4][0], place_quarter)
     plane_spread = start_spread(plane, eighth, stages[5])
     rhs_part[...] = finish_ordered(plane, rhs_first, rhs_ref, stages[6][0], rhs_plane)
     rhs_second = start_spread(depth, rhs_part, stages[7])
@@ -312,10 +363,11 @@
     def place_eighth(position, block):
         packed_ref[pl.ds(pl.multiple_of(position * width, width), width), :] = block
 
+    rhs_total[...] = finish_ordered(depth, rhs_second, rhs_part, stages[7][0], rhs_depth)
+    rhs_sides = start_sides(rhs_total, stages[9], count)
     finish_spread(plane, plane_spread, eighth, stages[5][0], place_eighth)
 
-    left, right = ties_ref[0:1, :], ties_ref[1:2, :]
-    row_ids = lax.broadcasted_iota(jnp.int32, (knots, lanes), 0)
+    row_ids = lax.broadcasted_iota(jnp.int32, (knots, 2 * lanes), 0)
     start = 0
     for group in range(knots // BLOCK):
         width = (group + 1) * BLOCK
@@ -343,46 +395,17 @@
 
     lax.fori_loop(0, knots, pivot, 0)
 
-    right_side = finish_ordered(depth, rhs_second, rhs_part, stages[7][0], rhs_depth)
+    right_side = finish_sides(rhs_sides, rhs_total, stages[9][0], count)
     base = DAMPING * applied(inverse, right_side, knots)
-    lane_ids = lax.broadcasted_iota(jnp.int32, (knots, lanes), 1)
-    first, last = lane_ids == 0, lane_ids == lanes - 1
-    me = lax.axis_index("tm")
-    has_before, has_after = me > 0, me < count - 1
-    after, before = lax.rem(me + 1, count), lax.rem(me + count - 1, count)
     change = base
-    for sweep in range(ITERS - 1):
-        sent[sweep] = change
-        ahead, behind = [
-            pltpu.make_async_remote_copy(
-                src_ref=sent.at[sweep],
-                dst_ref=land.at[sweep, side],
-                send_sem=send_sem.at[sweep, side],
-                recv_sem=recv_sem.at[sweep, side],
-                device_id={"tm": peer},
-                device_id_type=MESH,
-            )
-            for side, peer in enumerate((after, before))
-        ]
-        pl.when(has_after)(ahead.start)
-        pl.when(has_before)(behind.start)
-        own_low = jnp.where(first, 0.0, pltpu.roll(change, 1, 1))
-        own_high = jnp.where(last, 0.0, pltpu.roll(change, lanes - 1, 1))
-        pl.when(has_before)(ahead.wait_recv)
-        pl.when(has_after)(behind.wait_recv)
-        low, high = pltpu.roll(land[sweep, 0], 1, 1), pltpu.roll(land[sweep, 1], lanes - 1, 1)
-        low = jnp.where(jnp.logical_and(first, has_before), low, own_low)
-        high = jnp.where(jnp.logical_and(last, has_after), high, own_high)
-        tied = left * low + right * high
+    for _ in range(ITERS - 1):
+        tied = left * pltpu.roll(change, 1, 1) + right * pltpu.roll(change, 2 * lanes - 1, 1)
         change = (1.0 - DAMPING) * change + base + DAMPING * applied(inverse, tied, knots)
-        pl.when(has_after)(ahead.wait_send)
-        pl.when(has_before)(behind.wait_send)
-    o_ref[...] = change
+    o_ref[...] = change[:, :lanes]
 
 
 def updates(residuals, weights, partials, index, sources, blocks, ties, attitude, window, group):
     knots, lanes, count = attitude.shape[0], ties.shape[1], group[0]
-    sweeps = ITERS - 1
     plane, depth = along_plane(), along_depth()
     piece, whole, side = (PIECE, lanes), (depth[0] * PIECE, lanes), (knots, lanes)
 
@@ -404,27 +427,27 @@
             held(8, LOW),
             held(count, 8, LOW),
             held(depth[0], *piece),
-            held(*piece),
-            held(*whole),
-            held(plane[0] * whole[0], lanes),
+            held(PIECE + 8, lanes),
+            held(whole[0], 2 * lanes),
+            held(plane[0] * whole[0], 2 * lanes),
             held(*side),
             held(*side),
             held(plane[0], *side),
             held(depth[0], *side),
-            held(knots, *side),
-            held(sweeps, *side),
-            held(sweeps, 2, *side),
-            pltpu.SemaphoreType.DMA((sweeps, 2)),
-            pltpu.SemaphoreType.DMA((sweeps, 2)),
+            held(knots, knots, 2 * lanes),
+            held(PIECE, 2 * lanes),
+            held(*side),
         ]
         + stage_scratch(group, (ROWS, LOW))
         + stage_scratch(group, (8, LOW))
         + stage_scratch(plane, whole)
         + stage_scratch(depth, piece)
-        + stage_scratch(depth, piece)
-        + stage_scratch(plane, whole)
+        + stage_scratch(depth, (PIECE, 2 * lanes))
+        + stage_scratch(plane, (whole[0], 2 * lanes))
         + stage_scratch(plane, side)
-        + stage_scratch(depth, side),
+        + stage_scratch(depth, side)
+        + side_scratch((PIECE + 8, lanes))
+        + side_scratch(side),
         compiler_params=pltpu.CompilerParams(
             collective_id=1, has_side_effects=True, vmem_limit_bytes=48 << 20
         ),

time: 94.1 us -> 74.5 us (0.79)
  the two profiles are of different devices: /device:TPU:24 before, /device:TPU:1 now
where the time goes in v5:
time: 74.5 us; the launch traced here: 74.3 us
  Pallas kernels  60.9 us (82%)
  starting transfers between devices  4.54 us (6%)
  local copies, waits for them, and re-layouts  4.51 us (6%)
  matrix products  1.95 us (3%)
  other arithmetic  1.61 us (2%)
  between operations  0.78 us (1%)
    pallas_call x1, Pallas kernels, updates(): pl.pallas_call(functools.partial(update_kernel, knots, group), name='upda...  60.9 us
    ppermute x1, starting transfers between devices, on_device(): lax.ppermute(coupling[-1:], 'tm', [(i, i + 1) for i in range(times - 1)])  4.54 us
    unnamed x19, local copies, waits for them, and re-layouts  2.15 us
    dot_general x1, matrix products, on_device(): jnp.einsum('ktp,ltp->tkl', scaled.reshape(knot_count, tile_count, TILE),...  1.6 us
  transfers between devices with their start and end apart: 1, of which 0 were waited for; matrix products, arithmetic and copies ran while one was open for 4% of the time, Pallas kernels for 0%

profile of v5, /device:TPU:1, one launch (start us, length us, event | category | flops | bytes accessed | tf_op | source)
XLA Modules:
  0.0 74.3 jit_solution(5145303543437575644)
XLA Ops:
  0.6 1.2 %slice.22 = f32[1]{0:T(128)} slice(f32[128]{0:T(128)} %param.17), slice={[127:128]} | slice | bytes 8 | tf_op jit(solution)/shard_map/slice | solution.py:498
  1.9 4.5 %collective-permute-start = (f32[1]{0:T(128)}, f32[1]{0:T(128)}, u32[]{:S(2)}, u32[]{:S(2)}) collective-permute-start(f32[1]{0:T(128)} %slice.22), channel_id=1, source_target_pairs={{0,1},{1,2},{2,3},{3,4},{4,5},{5,6},{6,7},{7,8},{8,9},{9,10},{10,1... | collective-permute-start | bytes 20 | tf_op jit(solution)/shard_map/ppermute | solution.py:498
  6.4 1.6 %fusion.2 = f32[64,32,32]{2,1,0:T(8,128)S(1)} fusion(bf16[32,8192]{1,0:T(8,128)(2,1)} %attitude_ref.1, f32[8192]{0:T(1024)} %param.10), kind=kOutput, calls=%fused_computation.4 | convolution fusion | flops 17563648 | bytes 819200 | tf_op jit(solution)/shard_map/ktp,ltp->tkl/dot_general | solution.py:475
  8.0 0.3 copy.16
  8.4 0.2 fusion
  8.8 0.1 copy.20
  8.9 0.1 copy.19
  9.0 0.1 copy.18
  9.2 0.1 copy.17
  9.3 0.0 copy-start.8
  9.3 0.7 copy-done.8
  10.0 0.0 copy-start.7
  10.0 0.6 copy-done.7
  10.7 0.3 fusion.7
  11.0 0.0 copy-start
  11.0 0.0 copy-start.2
  11.0 0.0 copy-start.4
  11.0 0.0 copy-start.5
  11.1 0.0 copy-start.1
  11.1 0.0 collective-permute-done
  11.1 0.8 %maximum_bitcast_fusion = f32[1,128]{1,0:T(1,128)S(1)} fusion(f32[127]{0:T(128)S(1)} %bitcast.43, f32[1]{0:T(128)} %collective-permute-done), kind=kLoop, calls=%fused_computation.22 | loop fusion | flops 128 | bytes 1024 | tf_op jit(solution)/shard_map/stack | solution.py:510
  11.9 0.1 eq.17
  12.0 0.0 copy-done.3
  12.0 0.1 copy-done
  12.1 0.0 copy-done.2
  12.1 0.0 copy-done.4
  12.1 0.0 copy-done.5
  12.1 0.0 copy-done.1
  12.1 60.9 %updates.1 = (f32[5,4096]{1,0:T(8,128)S(1)}, f32[32,128]{1,0:T(8,128)S(1)}) custom-call(f32[1,8192]{1,0:T(1,128)S(1)} %bitcast.37, f32[1,8192]{1,0:T(1,128)S(1)} %bitcast.35, bf16[5,8192]{1,0:T(8,128)(2,1)S(1)} %copy-done.2, s32[1,8192]{1,0:T(1,128)S(1)} %bitcast.38, f32[5,4096]{1,0:T(8,128)S(1)} %copy-done.3, f32[8,96,128]{2,1,0:T(8,128)S(1)} %bitcast.34, ...), custom_call_target="tpu_custom_call" | custom-call | tf_op jit(solution)/shard_map/updates/pallas_call | solution.py:415
  73.0 0.0 copy-done.6
  73.0 0.6 bitcast_add_fusion.1
  73.6 0.7 copy.32
  (10 shorter events, 0.2 us)
Async XLA Ops:
  1.9 9.2 %collective-permute-start = (f32[1]{0:T(128)}, f32[1]{0:T(128)}, u32[]{:S(2)}, u32[]{:S(2)}) collective-permute-start(f32[1]{0:T(128)} %slice.22), channel_id=1, source_target_pairs={{0,1},{1,2},{2,3},{3,4},{4,5},{5,6},{6,7},{7,8},{8,9},{9,10},{10,1... | collective-permute-start | bytes 20 | tf_op jit(solution)/shard_map/ppermute | solution.py:498
  9.3 0.7 copy-start.8
  10.0 0.7 copy-start.7
  10.7 1.3 %copy-start.3 = (f32[5,4096]{1,0:T(8,128)S(1)}, f32[5,4096]{1,0:T(8,128)}, u32[]{:S(2)}) copy-start(f32[5,4096]{1,0:T(8,128)} %sources_ref.1) | copy-start | bytes 245764
  11.0 1.1 %copy-start = (bf16[32,8192]{1,0:T(8,128)(2,1)S(1)}, bf16[32,8192]{1,0:T(8,128)(2,1)}, u32[]{:S(2)}) copy-start(bf16[32,8192]{1,0:T(8,128)(2,1)} %attitude_ref.1) | copy-start | bytes 1572868
  11.0 1.1 %copy-start.2 = (bf16[5,8192]{1,0:T(8,128)(2,1)S(1)}, bf16[5,8192]{1,0:T(8,128)(2,1)}, u32[]{:S(2)}) copy-start(bf16[5,8192]{1,0:T(8,128)(2,1)} %partials_ref.1) | copy-start | bytes 245764
  11.0 1.1 %copy-start.4 = (f32[8192]{0:T(1024)S(1)}, f32[8192]{0:T(1024)}, u32[]{:S(2)}) copy-start(f32[8192]{0:T(1024)} %param.9) | copy-start | bytes 98308
  11.0 1.1 %copy-start.5 = (s32[8192]{0:T(1024)S(1)}, s32[8192]{0:T(1024)}, u32[]{:S(2)}) copy-start(s32[8192]{0:T(1024)} %param.13) | copy-start | bytes 98308
  11.1 1.0 %copy-start.1 = (f32[8192]{0:T(1024)S(1)}, f32[8192]{0:T(1024)}, u32[]{:S(2)}) copy-start(f32[8192]{0:T(1024)} %param.10) | copy-start | bytes 98308
  12.1 60.9 %copy-start.6 = (f32[128,32]{0,1:T(8,128)S(1)}, f32[128,32]{0,1:T(8,128)}, u32[]{:S(2)}) copy-start(f32[128,32]{0,1:T(8,128)} %param.16) | copy-start | bytes 49156

commit v6 on v5

--- a/solution.py
+++ b/solution.py
@@ -11,6 +11,7 @@
 ITERS = 8
 BLOCK = 8
 PIECE = 24
+USED = 20
 LOWER_PAIRS = tuple(((i, j) for i in range(5) for j in range(i + 1)))
 DAMPING = 0.8
 HIGHEST = lax.Precision.HIGHEST
@@ -254,6 +255,7 @@
     rhs_depth,
     inverse,
     wide_corner,
+    wide_quarters,
     rhs_total,
     *scratch,
 ):
@@ -287,18 +289,21 @@
         )
         return carry
 
-    lax.fori_loop(0, chunks, gather_sums, 0)
+    early = chunks * 5 // 8
+    lax.fori_loop(0, early, gather_sums, 0)
+    pl.semaphore_wait(barrier, peers)
+    plane_sum = start_sum(plane, blocks_ref, stages[2])
+    lax.fori_loop(early, chunks, gather_sums, 0)
     for h in range(count):
         start = 2 * ROWS * h
         moments[h] = total_ref[start : start + ROWS] + total_ref[start + ROWS : start + 2 * ROWS]
 
-    pl.semaphore_wait(barrier, peers)
-    plane_sum = start_sum(plane, blocks_ref, stages[2])
     time_sum = start_sum(group, moments, stages[0])
 
     total = finish_sum(plane, plane_sum, blocks_ref, stages[2][0])
     for part in range(depth[0]):
-        quarters[part] = total[PIECE * part : PIECE * (part + 1)]
+        quarters[part, :USED, :] = total[USED * part : USED * (part + 1)]
+        quarters[part, USED:, :] = jnp.zeros((PIECE - USED, total.shape[1]), jnp.float32)
     depth_sum = start_sum(depth, quarters, stages[3])
 
     total = finish_sum(group, time_sum, moments, stages[0][0])
@@ -308,7 +313,7 @@
     time_spread = start_spread(group, solved_ref, stages[1])
 
     corner[:PIECE, :] = finish_sum(depth, depth_sum, quarters, stages[3][0])
-    corner[PIECE:, :] = jnp.concatenate([ties_ref[...]] + [jnp.zeros_like(ties_ref[...])] * 3, axis=0)
+    corner[PIECE:, :] = jnp.broadcast_to(ties_ref[...], (8, ties_ref.shape[1]))
     corner_sides = start_sides(corner, stages[8], count)
 
     def place(position, block):
@@ -320,7 +325,10 @@
     wide = finish_sides(corner_sides, corner, stages[8][0], count)
     wide_corner[...] = wide[:PIECE]
     depth_spread = start_spread(depth, wide_corner, stages[4])
-    left, right = wide[PIECE : PIECE + 1], wide[PIECE + 1 : PIECE + 2]
+    right = wide[PIECE : PIECE + 1]
+    starts = lax.broadcasted_iota(jnp.int32, right.shape, 1) == 0
+    starts = jnp.logical_and(starts, lax.axis_index("tm") == 0)
+    left = jnp.where(starts, 0.0, pltpu.roll(jnp.broadcast_to(right, (8, right.shape[1])), 1, 1)[0:1])
     table = changes[...].reshape(count * 8, LOW)
     high, low = two_parts(table)
 
@@ -352,13 +360,15 @@
     rhs_first = start_spread(plane, rhs_ref, stages[6])
 
     def place_quarter(position, block):
-        eighth[pl.ds(pl.multiple_of(position * PIECE, PIECE), PIECE), :] = block
+        wide_quarters[position] = block
 
     finish_spread(depth, depth_spread, wide_corner, stages[4][0], place_quarter)
+    for part in range(depth[0]):
+        eighth[USED * part : USED * (part + 1), :] = wide_quarters[part, :USED, :]
     plane_spread = start_spread(plane, eighth, stages[5])
     rhs_part[...] = finish_ordered(plane, rhs_first, rhs_ref, stages[6][0], rhs_plane)
     rhs_second = start_spread(depth, rhs_part, stages[7])
-    width = depth[0] * PIECE
+    width = depth[0] * USED
 
     def place_eighth(position, block):
         packed_ref[pl.ds(pl.multiple_of(position * width, width), width), :] = block
@@ -407,7 +417,7 @@
 def updates(residuals, weights, partials, index, sources, blocks, ties, attitude, window, group):
     knots, lanes, count = attitude.shape[0], ties.shape[1], group[0]
     plane, depth = along_plane(), along_depth()
-    piece, whole, side = (PIECE, lanes), (depth[0] * PIECE, lanes), (knots, lanes)
+    piece, whole, side = (PIECE, lanes), (depth[0] * USED, lanes), (knots, lanes)
 
     def held(*shape):
         return pltpu.VMEM(shape, jnp.float32)
@@ -436,6 +446,7 @@
             held(depth[0], *side),
             held(knots, knots, 2 * lanes),
             held(PIECE, 2 * lanes),
+            held(depth[0], PIECE, 2 * lanes),
             held(*side),
         ]
         + stage_scratch(group, (ROWS, LOW))
@@ -493,10 +504,7 @@
     packed = lax.dot_general(
         tile_lower, selector, (((0,), (0,)), ((), ())), precision=HIGHEST
     )
-    packed = jnp.pad(packed, ((0, 768 - packed.shape[0]), (0, 0)))
-
-    earlier = lax.ppermute(coupling[-1:], "tm", [(i, i + 1) for i in range(times - 1)])
-    left = jnp.concatenate([earlier, coupling[:-1]])
+
     is_final = lax.axis_index("tm") == times - 1
     final_slot = lax.broadcasted_iota(jnp.int32, (window_count,), 0) == window_count - 1
     right = jnp.where(jnp.logical_and(is_final, final_slot), 0.0, coupling)
@@ -506,8 +514,8 @@
         source_partials,
         source_index,
         sources,
-        packed.reshape(8, 4 * PIECE, window_count),
-        jnp.stack([left, right]),
+        packed.reshape(8, 4 * USED, window_count),
+        right[None],
         attitude_partials,
         jnp.broadcast_to((tile_window - first_window)[:, None], (tile_count, TILE)).reshape(-1),
         time_group,

time: 74.5 us -> 66.4 us (0.89)
  the two profiles are of different devices: /device:TPU:1 before, /device:TPU:24 now
where the time goes in v6:
time: 66.4 us; the launch traced here: 65.2 us
  Pallas kernels  58.7 us (88%)
  local copies, waits for them, and re-layouts  2.93 us (4%)
  matrix products  1.95 us (3%)
  other arithmetic  0.84 us (1%)
  between operations  0.77 us (1%)
    pallas_call x1, Pallas kernels, updates(): pl.pallas_call(functools.partial(update_kernel, knots, group), name='upda...  58.7 us
    unnamed x19, local copies, waits for them, and re-layouts  1.84 us
    dot_general x1, matrix products, on_device(): jnp.einsum('ktp,ltp->tkl', scaled.reshape(knot_count, tile_count, TILE),...  1.61 us

profile of v6, /device:TPU:24, one launch (start us, length us, event | category | flops | bytes accessed | tf_op | source)
XLA Modules:
  0.0 65.2 jit_solution(14434120617483953606)
XLA Ops:
  0.6 1.6 %fusion.2 = f32[64,32,32]{2,1,0:T(8,128)S(1)} fusion(bf16[32,8192]{1,0:T(8,128)(2,1)} %attitude_ref.1, f32[8192]{0:T(1024)} %param.10), kind=kOutput, calls=%fused_computation.4 | convolution fusion | flops 17563648 | bytes 819200 | tf_op jit(solution)/shard_map/ktp,ltp->tkl/dot_general | solution.py:486
  2.2 0.3 copy.16
  2.6 0.2 fusion
  2.9 0.1 copy.20
  3.0 0.1 copy.19
  3.2 0.1 copy.18
  3.3 0.0 copy-start.7
  3.4 0.0 copy-start
  3.4 0.1 copy.17
  3.5 0.5 copy-done.7
  4.0 0.0 copy-start.2
  4.0 0.0 copy-start.3
  4.0 0.0 copy-start.4
  4.0 0.0 copy-start.5
  4.0 0.3 fusion.7
  4.4 0.0 copy-start.1
  4.4 0.1 eq.17
  4.5 0.0 copy-start.8
  4.5 0.7 %copy-done.8 = f32[128]{0:T(128)S(1)} copy-done((f32[128]{0:T(128)S(1)}, f32[128]{0:T(128)}, u32[]{:S(2)}) %copy-start.8) | copy-done | bytes 536
  5.2 0.0 copy-done
  5.2 0.0 copy-done.2
  5.2 0.0 copy-done.3
  5.2 0.0 copy-done.4
  5.2 0.0 copy-done.5
  5.2 0.0 copy-done.1
  5.2 0.0 copy-start.6
  5.2 58.7 %updates.1 = (f32[5,4096]{1,0:T(8,128)S(1)}, f32[32,128]{1,0:T(8,128)S(1)}) custom-call(f32[1,8192]{1,0:T(1,128)S(1)} %bitcast.34, f32[1,8192]{1,0:T(1,128)S(1)} %bitcast.32, bf16[5,8192]{1,0:T(8,128)(2,1)S(1)} %copy-done.2, s32[1,8192]{1,0:T(1,128)S(1)} %bitcast.35, f32[5,4096]{1,0:T(8,128)S(1)} %copy-done.3, f32[8,80,128]{2,1,0:T(8,128)S(1)} %bitcast.31, ...), custom_call_target="tpu_custom_call" | custom-call | tf_op jit(solution)/shard_map/updates/pallas_call | solution.py:425
  63.9 0.0 copy-done.6
  63.9 0.6 bitcast_add_fusion.1
  64.5 0.7 %copy.32 = f32[5,4096]{1,0:T(8,128)} copy(f32[5,4096]{1,0:T(8,128)S(1)} %get-tuple-element.8) | data formatting | bytes 163840
  (6 shorter events, 0.2 us)
Async XLA Ops:
  3.3 0.7 %copy-start.7 = (s32[64]{0:T(128)S(1)}, s32[64]{0:T(128)}, u32[]{:S(2)}) copy-start(s32[64]{0:T(128)} %param.14) | copy-start | bytes 772
  3.4 1.7 %copy-start = (bf16[32,8192]{1,0:T(8,128)(2,1)S(1)}, bf16[32,8192]{1,0:T(8,128)(2,1)}, u32[]{:S(2)}) copy-start(bf16[32,8192]{1,0:T(8,128)(2,1)} %attitude_ref.1) | copy-start | bytes 1572868
  4.0 1.1 %copy-start.2 = (bf16[5,8192]{1,0:T(8,128)(2,1)S(1)}, bf16[5,8192]{1,0:T(8,128)(2,1)}, u32[]{:S(2)}) copy-start(bf16[5,8192]{1,0:T(8,128)(2,1)} %partials_ref.1) | copy-start | bytes 245764
  4.0 1.1 %copy-start.3 = (f32[5,4096]{1,0:T(8,128)S(1)}, f32[5,4096]{1,0:T(8,128)}, u32[]{:S(2)}) copy-start(f32[5,4096]{1,0:T(8,128)} %sources_ref.1) | copy-start | bytes 245764
  4.0 1.1 %copy-start.4 = (f32[8192]{0:T(1024)S(1)}, f32[8192]{0:T(1024)}, u32[]{:S(2)}) copy-start(f32[8192]{0:T(1024)} %param.9) | copy-start | bytes 98308
  4.0 1.1 %copy-start.5 = (s32[8192]{0:T(1024)S(1)}, s32[8192]{0:T(1024)}, u32[]{:S(2)}) copy-start(s32[8192]{0:T(1024)} %param.13) | copy-start | bytes 98308
  4.4 0.8 %copy-start.1 = (f32[8192]{0:T(1024)S(1)}, f32[8192]{0:T(1024)}, u32[]{:S(2)}) copy-start(f32[8192]{0:T(1024)} %param.10) | copy-start | bytes 98308
  4.5 0.7 %copy-start.8 = (f32[128]{0:T(128)S(1)}, f32[128]{0:T(128)}, u32[]{:S(2)}) copy-start(f32[128]{0:T(128)} %param.17) | copy-start | bytes 1540
  5.2 58.7 %copy-start.6 = (f32[128,32]{0,1:T(8,128)S(1)}, f32[128,32]{0,1:T(8,128)}, u32[]{:S(2)}) copy-start(f32[128,32]{0,1:T(8,128)} %param.16) | copy-start | bytes 49156

commit v7 on v6

--- a/solution.py
+++ b/solution.py
@@ -321,7 +321,6 @@
         new_ref[:, span] = sources_ref[:, span] + block[:5]
         changes[position] = block
 
-    finish_spread(group, time_spread, solved_ref, stages[1][0], place)
     wide = finish_sides(corner_sides, corner, stages[8][0], count)
     wide_corner[...] = wide[:PIECE]
     depth_spread = start_spread(depth, wide_corner, stages[4])
@@ -329,6 +328,7 @@
     starts = lax.broadcasted_iota(jnp.int32, right.shape, 1) == 0
     starts = jnp.logical_and(starts, lax.axis_index("tm") == 0)
     left = jnp.where(starts, 0.0, pltpu.roll(jnp.broadcast_to(right, (8, right.shape[1])), 1, 1)[0:1])
+    finish_spread(group, time_spread, solved_ref, stages[1][0], place)
     table = changes[...].reshape(count * 8, LOW)
     high, low = two_parts(table)
 

time: 66.4 us -> 67.2 us (1.012)
  the two profiles are of different devices: /device:TPU:24 before, /device:TPU:1 now
where the time goes in v7:
time: 67.2 us; the launch traced here: 67 us
  Pallas kernels  60.5 us (90%)
  local copies, waits for them, and re-layouts  2.93 us (4%)
  matrix products  1.95 us (3%)
  other arithmetic  0.84 us (1%)
  between operations  0.77 us (1%)
    pallas_call x1, Pallas kernels, updates(): pl.pallas_call(functools.partial(update_kernel, knots, group), name='upda...  60.5 us
    unnamed x19, local copies, waits for them, and re-layouts  1.84 us
    dot_general x1, matrix products, on_device(): jnp.einsum('ktp,ltp->tkl', scaled.reshape(knot_count, tile_count, TILE),...  1.61 us

profile of v7, /device:TPU:1, one launch (start us, length us, event | category | flops | bytes accessed | tf_op | source)
XLA Modules:
  0.0 67.0 jit_solution(3500348026944218879)
XLA Ops:
  0.6 1.6 %fusion.2 = f32[64,32,32]{2,1,0:T(8,128)S(1)} fusion(bf16[32,8192]{1,0:T(8,128)(2,1)} %attitude_ref.1, f32[8192]{0:T(1024)} %param.10), kind=kOutput, calls=%fused_computation.4 | convolution fusion | flops 17563648 | bytes 819200 | tf_op jit(solution)/shard_map/ktp,ltp->tkl/dot_general | solution.py:486
  2.2 0.3 copy.16
  2.6 0.2 fusion
  2.9 0.1 copy.20
  3.0 0.1 copy.19
  3.2 0.1 copy.18
  3.3 0.0 copy-start.7
  3.4 0.0 copy-start
  3.4 0.1 copy.17
  3.5 0.5 copy-done.7
  4.0 0.0 copy-start.2
  4.0 0.0 copy-start.3
  4.0 0.0 copy-start.4
  4.0 0.0 copy-start.5
  4.0 0.3 fusion.7
  4.4 0.0 copy-start.1
  4.4 0.1 eq.17
  4.5 0.0 copy-start.8
  4.5 0.7 copy-done.8
  5.2 0.0 copy-done
  5.2 0.0 copy-done.2
  5.2 0.0 copy-done.3
  5.2 0.0 copy-done.4
  5.2 0.0 copy-done.5
  5.2 0.0 copy-done.1
  5.2 0.0 copy-start.6
  5.2 60.5 %updates.1 = (f32[5,4096]{1,0:T(8,128)S(1)}, f32[32,128]{1,0:T(8,128)S(1)}) custom-call(f32[1,8192]{1,0:T(1,128)S(1)} %bitcast.34, f32[1,8192]{1,0:T(1,128)S(1)} %bitcast.32, bf16[5,8192]{1,0:T(8,128)(2,1)S(1)} %copy-done.2, s32[1,8192]{1,0:T(1,128)S(1)} %bitcast.35, f32[5,4096]{1,0:T(8,128)S(1)} %copy-done.3, f32[8,80,128]{2,1,0:T(8,128)S(1)} %bitcast.31, ...), custom_call_target="tpu_custom_call" | custom-call | tf_op jit(solution)/shard_map/updates/pallas_call | solution.py:425
  65.8 0.0 copy-done.6
  65.8 0.6 bitcast_add_fusion.1
  66.4 0.7 copy.32
  (6 shorter events, 0.2 us)
Async XLA Ops:
  3.3 0.7 %copy-start.7 = (s32[64]{0:T(128)S(1)}, s32[64]{0:T(128)}, u32[]{:S(2)}) copy-start(s32[64]{0:T(128)} %param.14) | copy-start | bytes 772
  3.4 1.7 %copy-start = (bf16[32,8192]{1,0:T(8,128)(2,1)S(1)}, bf16[32,8192]{1,0:T(8,128)(2,1)}, u32[]{:S(2)}) copy-start(bf16[32,8192]{1,0:T(8,128)(2,1)} %attitude_ref.1) | copy-start | bytes 1572868
  4.0 1.1 %copy-start.2 = (bf16[5,8192]{1,0:T(8,128)(2,1)S(1)}, bf16[5,8192]{1,0:T(8,128)(2,1)}, u32[]{:S(2)}) copy-start(bf16[5,8192]{1,0:T(8,128)(2,1)} %partials_ref.1) | copy-start | bytes 245764
  4.0 1.1 %copy-start.3 = (f32[5,4096]{1,0:T(8,128)S(1)}, f32[5,4096]{1,0:T(8,128)}, u32[]{:S(2)}) copy-start(f32[5,4096]{1,0:T(8,128)} %sources_ref.1) | copy-start | bytes 245764
  4.0 1.1 %copy-start.4 = (f32[8192]{0:T(1024)S(1)}, f32[8192]{0:T(1024)}, u32[]{:S(2)}) copy-start(f32[8192]{0:T(1024)} %param.9) | copy-start | bytes 98308
  4.0 1.1 %copy-start.5 = (s32[8192]{0:T(1024)S(1)}, s32[8192]{0:T(1024)}, u32[]{:S(2)}) copy-start(s32[8192]{0:T(1024)} %param.13) | copy-start | bytes 98308
  4.4 0.8 %copy-start.1 = (f32[8192]{0:T(1024)S(1)}, f32[8192]{0:T(1024)}, u32[]{:S(2)}) copy-start(f32[8192]{0:T(1024)} %param.10) | copy-start | bytes 98308
  4.5 0.7 copy-start.8
  5.2 60.6 %copy-start.6 = (f32[128,32]{0,1:T(8,128)S(1)}, f32[128,32]{0,1:T(8,128)}, u32[]{:S(2)}) copy-start(f32[128,32]{0,1:T(8,128)} %param.16) | copy-start | bytes 49156
